TPU v7x, 256 devices: a whole 4x4x8 slice. The times are simulated.
256 devices in a mesh: row: 32 (over y, x, core), col: 8 (over z).
Axes of the slice: x: 4, y: 4, z: 8, core: 2. Of those that a mesh axis runs over, the one named last changes fastest.
Arguments:
- diag: float32 [4, 1024, 1024], P(None, 'row'), as said below
- panel_rows: float32 [64, 8, 64, 1024], P('row', None, None, 'col')
- panel_cols: float32 [8, 8, 64, 1024], P('col', None, 'row')
- trailing: float32 [64, 8, 8, 64, 1024], P('row', 'col')
- sketch: float32 [64, 1024], replicated, may hold values from -6 to 6
- panel_rank: int32 [64], P('row'), may hold values from 16 to 64
- col_rank: int32 [8], P('col'), may hold values from 16 to 64
- tile_rank: int32 [64, 8], P('row', 'col'), may hold values from 32 to 64
- keep_rank: int32 [64, 8], P('row', 'col'), may hold values from 8 to 32
Outputs:
- new_tiles: float32 [64, 8, 8, 64, 1024], P('row', 'col')
Inputs may be any that keep to these rules, and one draw needn't show every extreme that they name: `keep_rank`: recompression ranks, never above the tile's rank. diag[0] is symmetric positive definite with smallest eigenvalue 0.5 or more; the tangents are symmetric.
All inputs are finite; a program needn't handle non-finite values.
Results may differ from a plain program's by a relative error of at most 0.0003.
Values sent between devices are 32-bit elements; how exact they have to be, the bound alone decides.
A program may use at most 192 MiB of HBM per device.

v0:
```python
import math

import jax
import jax.numpy as jnp
from jax import lax
from jax.sharding import PartitionSpec as P

HIGHEST_PRECISION = lax.Precision.HIGHEST


def highest_accuracy(left, right):
    return jnp.dot(left, right, precision=HIGHEST_PRECISION, preferred_element_type=jnp.float32)


def rank_mask(rank_values, rank_count):
    return (jnp.arange(rank_count, dtype=jnp.int32) < rank_values[..., None]).astype(jnp.float32)


def inverse_apply(lower_factor, rank_rows):
    half_solved = jax.scipy.linalg.solve_triangular(lower_factor, rank_rows.T, lower=True)
    full_solved = jax.scipy.linalg.solve_triangular(lower_factor, half_solved, lower=True, trans=1)
    return full_solved.T


def sketch_apply(active_sketch, previous_left_factor, previous_right_factor, u_row, mix_in, u_col):
    return highest_accuracy(
        highest_accuracy(active_sketch, previous_right_factor.T), previous_left_factor
    ) - highest_accuracy(
        highest_accuracy(highest_accuracy(active_sketch, u_col.T), mix_in.T), u_row
    )


def basis_apply(
    row_basis_matrix, previous_left_factor, previous_right_factor, u_row, mix_in, u_col
):
    return highest_accuracy(
        highest_accuracy(row_basis_matrix, previous_left_factor.T), previous_right_factor
    ) - highest_accuracy(
        highest_accuracy(highest_accuracy(row_basis_matrix, u_row.T), mix_in), u_col
    )


def compress_all(
    previous_left_factor,
    previous_right_factor,
    u_row,
    mix_in,
    u_col,
    du_old,
    dv_old,
    du_row,
    dmix_in,
    du_col,
    active_sketch,
    live_mask,
):
    sketched = sketch_apply(
        active_sketch, previous_left_factor, previous_right_factor, u_row, mix_in, u_col
    )
    gram_matrix = highest_accuracy(sketched, sketched.T) + jnp.diag(1.0 - live_mask)
    factor = jnp.linalg.cholesky(gram_matrix)
    row_basis_matrix = jax.scipy.linalg.solve_triangular(factor, sketched, lower=True)
    coefficients = basis_apply(
        row_basis_matrix, previous_left_factor, previous_right_factor, u_row, mix_in, u_col
    )
    up_scale = math.sqrt(previous_left_factor.shape[1])
    down_scale = math.sqrt(previous_left_factor.shape[0])

    def tangent_direction(
        previous_left_derivative,
        previous_right_derivative,
        row_left_derivative,
        mixing_derivative,
        column_left_derivative,
    ):
        sketch_derivative = highest_accuracy(
            highest_accuracy(active_sketch, previous_right_derivative.T), previous_left_factor
        ) + highest_accuracy(
            highest_accuracy(active_sketch, previous_right_factor.T), previous_left_derivative
        )
        sketch_derivative = sketch_derivative - highest_accuracy(
            highest_accuracy(highest_accuracy(active_sketch, column_left_derivative.T), mix_in.T),
            u_row,
        )
        sketch_derivative = sketch_derivative - highest_accuracy(
            highest_accuracy(highest_accuracy(active_sketch, u_col.T), mixing_derivative.T), u_row
        )
        sketch_derivative = sketch_derivative - highest_accuracy(
            highest_accuracy(highest_accuracy(active_sketch, u_col.T), mix_in.T),
            row_left_derivative,
        )
        d_gram = highest_accuracy(sketch_derivative, sketched.T) + highest_accuracy(
            sketched, sketch_derivative.T
        )
        inner = jax.scipy.linalg.solve_triangular(factor, d_gram, lower=True)
        middle = jax.scipy.linalg.solve_triangular(factor, inner.T, lower=True)
        lower_part = jnp.tril(middle) - 0.5 * jnp.diag(jnp.diagonal(middle))
        d_factor = highest_accuracy(factor, lower_part)
        d_basis = jax.scipy.linalg.solve_triangular(
            factor, sketch_derivative - highest_accuracy(d_factor, row_basis_matrix), lower=True
        )
        coefficient_derivative = basis_apply(
            d_basis, previous_left_factor, previous_right_factor, u_row, mix_in, u_col
        )
        coefficient_derivative = (
            coefficient_derivative
            + highest_accuracy(
                highest_accuracy(row_basis_matrix, previous_left_derivative.T),
                previous_right_factor,
            )
            + highest_accuracy(
                highest_accuracy(row_basis_matrix, previous_left_factor.T),
                previous_right_derivative,
            )
        )
        coefficient_derivative = coefficient_derivative - highest_accuracy(
            highest_accuracy(highest_accuracy(row_basis_matrix, row_left_derivative.T), mix_in),
            u_col,
        )
        coefficient_derivative = coefficient_derivative - highest_accuracy(
            highest_accuracy(highest_accuracy(row_basis_matrix, u_row.T), mixing_derivative), u_col
        )
        coefficient_derivative = coefficient_derivative - highest_accuracy(
            highest_accuracy(highest_accuracy(row_basis_matrix, u_row.T), mix_in),
            column_left_derivative,
        )
        return (d_basis * up_scale, coefficient_derivative / down_scale)

    tangent_basis, tangent_coeff = jax.vmap(tangent_direction)(
        du_old, dv_old, du_row, dmix_in, du_col
    )
    return (row_basis_matrix * up_scale, coefficients / down_scale, tangent_basis, tangent_coeff)


def update_tile(
    row_tile, row_solved, col_tile, col_solved, col_products, old_tile, tile_mask, keep_mask, sketch
):
    old_tile = old_tile * tile_mask[None, :, None]
    mixing = highest_accuracy(row_tile[4], col_solved.T)
    tangent_mix = jnp.stack(
        [
            highest_accuracy(row_tile[5 + direction], col_solved.T)
            + highest_accuracy(row_solved, col_tile[5 + direction].T)
            - highest_accuracy(row_solved, col_products[direction].T)
            for direction in range(3)
        ]
    )
    active_sketch = sketch * keep_mask[:, None]
    basis_out, coeff_out, tangent_basis, tangent_coeff = compress_all(
        old_tile[0],
        old_tile[4],
        row_tile[0],
        mixing,
        col_tile[0],
        old_tile[1:4],
        old_tile[5:8],
        row_tile[1:4],
        tangent_mix,
        col_tile[1:4],
        active_sketch,
        keep_mask,
    )
    return jnp.concatenate([basis_out[None], tangent_basis, coeff_out[None], tangent_coeff], axis=0)


def on_device(
    diag, panel_rows, panel_cols, trailing, sketch, panel_rank, col_rank, tile_rank, keep_rank
):
    rank_count = sketch.shape[0]
    tile_width = sketch.shape[1]
    gathered = lax.all_gather(diag, "row", axis=1, tiled=True)
    primal = gathered[0]
    lower_factor = jnp.linalg.cholesky(primal)
    rows_kept = (
        lax.all_gather(panel_rows, "col", axis=3, tiled=True)
        * rank_mask(panel_rank, rank_count)[:, None, :, None]
    )
    cols_kept = (
        lax.all_gather(panel_cols, "row", axis=2, tiled=True)
        * rank_mask(col_rank, rank_count)[:, None, :, None]
    )
    col_tile = cols_kept[0]
    col_solved = inverse_apply(lower_factor, col_tile[4])
    col_products = jnp.einsum("aj,tij->tai", col_solved, gathered[1:], precision=HIGHEST_PRECISION)
    local_rows = rows_kept.shape[0]
    row_solved = inverse_apply(lower_factor, rows_kept[:, 4].reshape(-1, tile_width)).reshape(
        local_rows, rank_count, tile_width
    )
    tile_live = rank_mask(tile_rank[:, 0], rank_count)
    keep_live = rank_mask(keep_rank[:, 0], rank_count)

    def one_tile(row_tile, row_z, old_tile, tile_mask, keep_mask):
        return update_tile(
            row_tile,
            row_z,
            col_tile,
            col_solved,
            col_products,
            old_tile,
            tile_mask,
            keep_mask,
            sketch,
        )

    updated = jax.vmap(one_tile)(rows_kept, row_solved, trailing[:, 0], tile_live, keep_live)
    return updated[:, None]


def solution(mesh):
    in_specs = (
        P(None, "row", None),
        P("row", None, None, "col"),
        P("col", None, "row", None),
        P("row", "col", None, None, None),
        P(),
        P("row"),
        P("col"),
        P("row", "col"),
        P("row", "col"),
    )
    out_specs = P("row", "col", None, None, None)
    return jax.shard_map(
        on_device, mesh=mesh, in_specs=in_specs, out_specs=out_specs, check_vma=False
    )
```

profile of v0, /device:TPU:1, one launch (start us, length us, event | category | flops | bytes accessed | tf_op | source)
XLA Modules:
  0.0 733.9 jit_solution(14539865115307290714)
XLA Ops:
  28.6 34.0 %all-gather.4.cloned.1.call-done = f32[1,8,64,1024]{3,1,0,2:T(8,128)} async-done(((f32[1,8,2,1024]{3,1,0,2:T(8,128)}), f32[1,8,64,1024]{3,1,0,2:T(8,128)}) %all-gather.4.cloned.1.call-update) | async-done | bytes 2097168 | tf_op jit(solution)/shard_map/all_gather | solution.py:179
  68.1 54.0 %all-gather.6.cloned.1.call-done = f32[2,8,64,1024]{3,2,0,1:T(8,128)} async-done(((f32[2,8,64,128]{3,2,0,1:T(8,128)}), f32[2,8,64,1024]{3,2,0,1:T(8,128)}) %all-gather.6.cloned.1.call-update) | async-done | bytes 4194320 | tf_op jit(solution)/shard_map/all_gather | solution.py:175
  130.6 74.5 %all-gather.8.cloned.1.call-done = f32[4,1024,1024]{2,0,1:T(4,128)} async-done(((f32[4,32,1024]{2,0,1:T(4,128)}), f32[4,1024,1024]{2,0,1:T(4,128)}) %all-gather.8.cloned.1.call-update) | async-done | bytes 16777232 | tf_op jit(solution)/shard_map/all_gather | solution.py:171
  205.1 8.7 %slice.584 = f32[1,1024,1024]{2,0,1:T(1,128)} slice(f32[4,1024,1024]{2,0,1:T(4,128)} %all-gather.8.cloned.1.call-done), slice={[0:1], [0:1024], [0:1024]} | slice | bytes 8388608 | tf_op jit(solution)/shard_map/slice | solution.py:172
  213.8 11.4 %copy.214 = f32[1,1024,1024]{1,2,0:T(8,128)} copy(f32[1,1024,1024]{2,0,1:T(1,128)} %slice.584) | data formatting | bytes 8388608
  225.2 5.0 fusion.2
  232.2 11.7 %cholesky.241 = f32[128,128]{1,0:T(8,128)S(1)} custom-call(f32[128,128]{1,0:T(8,128)S(1)} %cholesky.622), custom_call_target="Cholesky" | custom-call | tf_op jit(solution)/shard_map/jit(cholesky)/cholesky | solution.py:173
  243.9 9.8 %custom-call.86 = f32[1,128,128]{1,2,0:T(8,128)S(1)} custom-call(f32[1,128,128]{2,1,0:T(8,128)S(1)} %get-tuple-element.70), custom_call_target="InvertDiagBlocksLowerTriangular" | custom-call | tf_op jit(solution)/shard_map/jit(cholesky)/cholesky | solution.py:173
  260.2 11.8 %cholesky.264 = f32[128,128]{1,0:T(8,128)S(1)} custom-call(f32[128,128]{1,0:T(8,128)S(1)} %cholesky.626), custom_call_target="Cholesky" | custom-call | tf_op jit(solution)/shard_map/jit(cholesky)/cholesky | solution.py:173
  272.7 9.8 %custom-call.87 = f32[1,128,128]{1,2,0:T(8,128)S(1)} custom-call(f32[1,128,128]{2,1,0:T(8,128)S(1)} %get-tuple-element.67), custom_call_target="InvertDiagBlocksLowerTriangular" | custom-call | tf_op jit(solution)/shard_map/jit(cholesky)/cholesky | solution.py:173
  285.8 11.7 %cholesky.502 = f32[128,128]{1,0:T(8,128)S(1)} custom-call(f32[128,128]{1,0:T(8,128)S(1)} %cholesky.631), custom_call_target="Cholesky" | custom-call | tf_op jit(solution)/shard_map/jit(cholesky)/cholesky | solution.py:173
  298.8 9.8 %custom-call.88 = f32[1,128,128]{1,2,0:T(8,128)S(1)} custom-call(f32[1,128,128]{2,1,0:T(8,128)S(1)} %get-tuple-element.64), custom_call_target="InvertDiagBlocksLowerTriangular" | custom-call | tf_op jit(solution)/shard_map/jit(cholesky)/cholesky | solution.py:173
  312.1 11.9 %cholesky.521 = f32[128,128]{1,0:T(8,128)S(1)} custom-call(f32[128,128]{1,0:T(8,128)S(1)} %cholesky.636), custom_call_target="Cholesky" | custom-call | tf_op jit(solution)/shard_map/jit(cholesky)/cholesky | solution.py:173
  325.3 9.8 %custom-call.89 = f32[1,128,128]{1,2,0:T(8,128)S(1)} custom-call(f32[1,128,128]{2,1,0:T(8,128)S(1)} %get-tuple-element.61), custom_call_target="InvertDiagBlocksLowerTriangular" | custom-call | tf_op jit(solution)/shard_map/jit(cholesky)/cholesky | solution.py:173
  338.5 11.7 %cholesky.540 = f32[128,128]{1,0:T(8,128)S(1)} custom-call(f32[128,128]{1,0:T(8,128)S(1)} %cholesky.641), custom_call_target="Cholesky" | custom-call | tf_op jit(solution)/shard_map/jit(cholesky)/cholesky | solution.py:173
  351.5 10.2 %custom-call.90 = f32[1,128,128]{1,2,0:T(8,128)S(1)} custom-call(f32[1,128,128]{2,1,0:T(8,128)S(1)} %get-tuple-element.58), custom_call_target="InvertDiagBlocksLowerTriangular" | custom-call | tf_op jit(solution)/shard_map/jit(cholesky)/cholesky | solution.py:173
  365.0 11.7 %cholesky.560 = f32[128,128]{1,0:T(8,128)S(1)} custom-call(f32[128,128]{1,0:T(8,128)S(1)} %cholesky.646), custom_call_target="Cholesky" | custom-call | tf_op jit(solution)/shard_map/jit(cholesky)/cholesky | solution.py:173
  378.1 9.8 %custom-call.91 = f32[1,128,128]{1,2,0:T(8,128)S(1)} custom-call(f32[1,128,128]{2,1,0:T(8,128)S(1)} %get-tuple-element.55), custom_call_target="InvertDiagBlocksLowerTriangular" | custom-call | tf_op jit(solution)/shard_map/jit(cholesky)/cholesky | solution.py:173
  390.9 11.9 %cholesky.580 = f32[128,128]{1,0:T(8,128)S(1)} custom-call(f32[128,128]{1,0:T(8,128)S(1)} %cholesky.651), custom_call_target="Cholesky" | custom-call | tf_op jit(solution)/shard_map/jit(cholesky)/cholesky | solution.py:173
  404.0 9.8 %custom-call.92 = f32[1,128,128]{1,2,0:T(8,128)S(1)} custom-call(f32[1,128,128]{2,1,0:T(8,128)S(1)} %get-tuple-element.52), custom_call_target="InvertDiagBlocksLowerTriangular" | custom-call | tf_op jit(solution)/shard_map/jit(cholesky)/cholesky | solution.py:173
  416.5 11.7 %cholesky.598 = f32[128,128]{1,0:T(8,128)S(1)} custom-call(f32[128,128]{1,0:T(8,128)S(1)} %convolution_subtract_fusion.21), custom_call_target="Cholesky" | custom-call | tf_op jit(solution)/shard_map/jit(cholesky)/cholesky | solution.py:173
  435.0 4.9 select_select_fusion
  439.9 28.2 %while.1 = (s32[]{:T(128)}, f32[1024,1024]{1,0:T(8,128)}, s32[8,2]{0,1:T(2,128)S(1)}, f32[8,128,128]{2,1,0:T(8,128)}, s32[]{:T(128)}) while((s32[]{:T(128)}, f32[1024,1024]{1,0:T(8,128)}, s32[8,2]{0,1:T(2,128)S(1)}, f32[8,128,128]{2,1,0:T(8,128)}, s32[]{:T(128)}) %tuple.84), condition=%wide.while_cond, body=%wide.while_body.sunk | while | flops 2 | bytes 132705 | solution.py:21
  468.1 79.6 %custom-call.93 = f32[8,128,128]{1,2,0:T(8,128)S(1)} custom-call(f32[8,128,128]{2,1,0:T(8,128)} %get-tuple-element.13), custom_call_target="InvertDiagBlocksLowerTriangular" | custom-call | tf_op jit(solution)/shard_map/jit(_solve_triangular)/triangular_solve | solution.py:21
  574.2 11.7 %custom-call.94 = f32[2,64,64]{2,1,0:T(8,128)S(1)} custom-call(f32[2,64,64]{2,1,0:T(8,128)S(1)} %fusion.264), custom_call_target="Cholesky" | custom-call | tf_op jit(solution)/shard_map/vmap(jit(cholesky))/cholesky | solution.py:61
  586.2 10.2 %custom-call.95 = f32[2,1,64,64]{2,3,1,0:T(8,128)S(1)} custom-call(f32[2,1,64,64]{3,2,1,0:T(8,128)S(1)} %select_bitcast_fusion), custom_call_target="InvertDiagBlocksLowerTriangular" | custom-call | tf_op jit(solution)/shard_map/vmap(jit(_solve_triangular))/triangular_solve | solution.py:62
  619.8 9.7 %slice.592 = f32[3,1024,1024]{2,0,1:T(4,128)S(1)} slice(f32[4,1024,1024]{2,0,1:T(4,128)} %all-gather.8.cloned.1.call-done), slice={[1:4], [0:1024], [0:1024]} | slice | bytes 25165824 | tf_op jit(solution)/shard_map/slice | solution.py:184
  629.5 20.2 %fusion.23 = f32[3,64,1024]{2,1,0:T(8,128)S(1)} fusion(f32[3,1024,1024]{2,0,1:T(4,128)S(1)} %slice.592, f32[1024,64]{0,1:T(8,128)S(1)} %constant_dynamic-update-slice_fusion.36), kind=kOutput, calls=%fused_computation.33 | convolution fusion | flops 2415919104 | bytes 13631488 | tf_op jit(solution)/shard_map/aj,tij->tai/dot_general | solution.py:184
  670.8 4.4 copy.177
  681.2 5.3 copy.179
  686.5 5.3 fusion.3
  695.2 4.2 copy.183
  (318 shorter events, 206.7 us)
Async XLA Ops:
  6.5 56.1 %all-gather.4.cloned.1.call-start = ((), (), s32[]{:S(2)}) async-start(), calls=%async_computation | async-start | bytes 2162688 | tf_op jit(solution)/shard_map/all_gather | solution.py:179
  8.0 114.1 %all-gather.6.cloned.1.call-start = ((), (), s32[]{:S(2)}) async-start(), calls=%async_computation.1 | async-start | bytes 4718592 | tf_op jit(solution)/shard_map/all_gather | solution.py:175
  10.0 195.1 %all-gather.8.cloned.1.call-start = ((), (), s32[]{:S(2)}) async-start(), calls=%async_computation.2 | async-start | bytes 17301504 | tf_op jit(solution)/shard_map/all_gather | solution.py:171
  17.1 3.2 copy-start.12
  20.2 5.9 copy-start.1
  20.9 3.1 copy-start.13
  65.5 1.4 copy-start.3
  66.9 504.7 %copy-start.15 = (f32[2,64,64]{2,1,0:T(8,128)}, f32[2,64,64]{2,1,0:T(8,128)S(1)}, u32[]{:S(2)}) copy-start(f32[2,64,64]{2,1,0:T(8,128)S(1)} %fusion.38) | copy-start | bytes 98308
  124.9 2.0 copy-start.2
  230.2 2.0 copy-start.5
  563.2 10.9 %copy-start.27 = (pred[64,64]{1,0:T(8,128)(4,1)S(1)}, pred[64,64]{1,0:T(8,128)(4,1)}, u32[]{:S(2)}) copy-start(pred[64,64]{1,0:T(8,128)(4,1)} %get-tuple-element.120) | copy-start | bytes 12292
  564.5 21.6 %copy-start.25 = (pred[64,64]{1,0:T(8,128)(4,1)S(1)}, pred[64,64]{1,0:T(8,128)(4,1)}, u32[]{:S(2)}) copy-start(pred[64,64]{1,0:T(8,128)(4,1)} %iota_compare_fusion.5) | copy-start | bytes 12292
  571.8 14.3 %copy-start.18 = (f32[2,64,64]{2,1,0:T(8,128)}, f32[2,64,64]{2,1,0:T(8,128)S(1)}, u32[]{:S(2)}) copy-start(f32[2,64,64]{2,1,0:T(8,128)S(1)} %fusion.331) | copy-start | bytes 98308
  585.9 23.7 %copy-start.20 = (f32[2,64,64]{2,1,0:T(8,128)}, f32[2,64,64]{2,1,0:T(8,128)S(1)}, u32[]{:S(2)}) copy-start(f32[2,64,64]{2,1,0:T(8,128)S(1)} %custom-call.94) | copy-start | bytes 98308
  596.4 11.8 %copy-start = (f32[1024,1024]{1,0:T(8,128)S(1)}, f32[1024,1024]{1,0:T(8,128)}, u32[]{:S(2)}) copy-start(f32[1024,1024]{1,0:T(8,128)} %get-tuple-element.169) | copy-start | bytes 12582916
  629.4 20.2 %copy-start.24 = (f32[2,64,64]{2,1,0:T(8,128)S(1)}, f32[2,64,64]{2,1,0:T(8,128)}, u32[]{:S(2)}) copy-start(f32[2,64,64]{2,1,0:T(8,128)} %fusion.54) | copy-start | bytes 98308
  629.4 21.8 %copy-start.23 = (f32[2,64,64]{2,1,0:T(8,128)S(1)}, f32[2,64,64]{2,1,0:T(8,128)}, u32[]{:S(2)}) copy-start(f32[2,64,64]{2,1,0:T(8,128)} %fusion.53) | copy-start | bytes 98308
  629.4 24.6 %copy-start.22 = (f32[2,64,64]{2,1,0:T(8,128)S(1)}, f32[2,64,64]{2,1,0:T(8,128)}, u32[]{:S(2)}) copy-start(f32[2,64,64]{2,1,0:T(8,128)} %fusion.52) | copy-start | bytes 98308
  649.6 6.5 copy-start.16
  651.2 8.1 %copy-start.11 = (f32[2,3,64,1024]{3,2,0,1:T(8,128)S(1)}, f32[2,3,64,1024]{3,2,0,1:T(8,128)}, u32[]{:S(2)}) copy-start(f32[2,3,64,1024]{3,2,0,1:T(8,128)} %get-tuple-element.28) | copy-start | bytes 4718596
  651.2 8.1 %copy-start.19 = (f32[2,64,64]{2,1,0:T(8,128)S(1)}, f32[2,64,64]{2,1,0:T(8,128)}, u32[]{:S(2)}) copy-start(f32[2,64,64]{2,1,0:T(8,128)} %copy-done.18) | copy-start | bytes 98308
  656.7 7.0 copy-start.7
  656.7 7.0 copy-start.9
  656.7 7.0 copy-start.14
  667.1 11.2 %copy-start.21 = (f32[2,64,64]{2,1,0:T(8,128)S(1)}, f32[2,64,64]{2,1,0:T(8,128)}, u32[]{:S(2)}) copy-start(f32[2,64,64]{2,1,0:T(8,128)} %copy-done.20) | copy-start | bytes 98308
  667.1 11.2 %copy-start.26 = (pred[64,64]{1,0:T(8,128)(4,1)S(1)}, pred[64,64]{1,0:T(8,128)(4,1)}, u32[]{:S(2)}) copy-start(pred[64,64]{1,0:T(8,128)(4,1)} %iota_compare_fusion.5) | copy-start | bytes 12292
  701.9 4.5 copy-start.17
  701.9 4.7 copy-start.4
  706.6 6.1 copy-start.10
  712.6 5.3 copy-start.8
  714.8 7.6 %copy-start.6 = (f32[2,3,64,1024]{3,2,0,1:T(8,128)S(1)}, f32[2,3,64,1024]{3,2,0,1:T(8,128)}, u32[]{:S(2)}) copy-start(f32[2,3,64,1024]{3,2,0,1:T(8,128)} %get-tuple-element.24) | copy-start | bytes 4718596
Sparse Core Ops, SparseCore 0:
  9.9 52.7 all-gather.3
  64.4 57.7 all-gather.5
  124.7 80.3 all-gather.7
where the time goes:
time: 744 us; the launch traced here: 734 us
  other arithmetic  299 us (40%)
  waiting for transfers between devices  163 us (22%)
  matrix products  152 us (20%)
  local copies, waits for them, and re-layouts  98.7 us (13%)
  between operations  20.8 us (3%)
    another operation x30, other arithmetic, on_device(): lower_factor = jnp.linalg.cholesky(primal)  172 us
    another operation x3, other arithmetic, inverse_apply(): jax.scipy.linalg.solve_triangular(lower_factor, half_solved, lower=True,...  84.5 us
    all_gather x1, waiting for transfers between devices, on_device(): gathered = lax.all_gather(diag, 'row', axis=1, tiled=True)  74.5 us
    dot_general x48, matrix products, highest_accuracy(): jnp.dot(left, right, precision=HIGHEST_PRECISION, preferred_element_type=...  69.4 us
    all_gather x1, waiting for transfers between devices, on_device(): lax.all_gather(panel_rows, 'col', axis=3, tiled=True)  54 us
    all_gather x1, waiting for transfers between devices, on_device(): lax.all_gather(panel_cols, 'row', axis=2, tiled=True)  34 us
    another operation x24, local copies, waits for them, and re-layouts  28.2 us
    another operation x14, matrix products, on_device(): lower_factor = jnp.linalg.cholesky(primal)  22.9 us
  transfers between devices with their start and end apart: 3, of which 3 were waited for; matrix products, arithmetic and copies ran while one was open for 4% of the time, Pallas kernels for 0%

commit v1 on v0

v1 whole, which is shorter than its diff:
```python
import functools
import math

import jax
import jax.numpy as jnp
from jax import lax
from jax.experimental import pallas as pl
from jax.experimental.pallas import tpu as pltpu
from jax.sharding import PartitionSpec as P

HI = lax.Precision.HIGHEST
BLOCK = 128
NPIV = 8
LIVE = 32
F32 = jnp.float32


def nn(x, y):
    return lax.dot_general(
        x, y, (((1,), (0,)), ((), ())), precision=HI, preferred_element_type=F32
    )


def nt(x, y):
    return lax.dot_general(
        x, y, (((1,), (1,)), ((), ())), precision=HI, preferred_element_type=F32
    )


def total(terms):
    terms = list(terms)
    while len(terms) > 1:
        terms = [
            terms[i] + terms[i + 1] if i + 1 < len(terms) else terms[i]
            for i in range(0, len(terms), 2)
        ]
    return terms[0]


def small_inverse(m):
    n = len(m)
    if n == 1:
        return [[1.0 / m[0][0]]]
    if n == 2:
        r = 1.0 / (m[0][0] * m[1][1] - m[0][1] * m[0][1])
        return [[m[1][1] * r, -m[0][1] * r], [-m[0][1] * r, m[0][0] * r]]
    h = n // 2
    e = small_inverse([row[:h] for row in m[:h]])
    b = [row[h:] for row in m[:h]]
    x = [[total(e[i][k] * b[k][j] for k in range(h)) for j in range(h)] for i in range(h)]
    s = [[None] * h for _ in range(h)]
    for i in range(h):
        for j in range(i, h):
            s[i][j] = m[h + i][h + j] - total(b[k][i] * x[k][j] for k in range(h))
            s[j][i] = s[i][j]
    g = small_inverse(s)
    o = [[-total(x[i][k] * g[k][j] for k in range(h)) for j in range(h)] for i in range(h)]
    t = [[None] * h for _ in range(h)]
    for i in range(h):
        for j in range(i, h):
            t[i][j] = e[i][j] - total(o[i][k] * x[j][k] for k in range(h))
            t[j][i] = t[i][j]
    return [t[i] + o[i] for i in range(h)] + [[o[j][i] for j in range(h)] + g[i] for i in range(h)]


def block_inverse(d):
    n = d.shape[0]
    lane = lax.broadcasted_iota(jnp.int32, (n, n), 1)
    sub = lax.broadcasted_iota(jnp.int32, (n, n), 0)
    lane8 = lax.broadcasted_iota(jnp.int32, (8, n), 1)
    for j in range(0, n, NPIV):
        m = [[None] * NPIV for _ in range(NPIV)]
        for r in range(NPIV):
            for c in range(r, NPIV):
                m[r][c] = jnp.broadcast_to(d[j + r : j + r + 1, j + c : j + c + 1], (8, n))
                m[c][r] = m[r][c]
        cols = [jnp.broadcast_to(d[:, j + q : j + q + 1], (n, n)) for q in range(NPIV)]
        p = small_inverse(m)
        own = (lane8 >= j) & (lane8 < j + NPIV)
        rows = [
            jnp.where(own, (lane8 == j + q).astype(F32), jnp.broadcast_to(d[j + q : j + q + 1, :], (8, n)))
            for q in range(NPIV)
        ]
        new = [total(p[q][k] * rows[k] for k in range(NPIV)) for q in range(NPIV)]
        new = [jnp.concatenate([t] * (n // 8), axis=0) for t in new]
        out = jnp.where((lane >= j) & (lane < j + NPIV), 0.0, d)
        for q in range(NPIV):
            out = out - cols[q] * new[q]
        for q in range(NPIV):
            out = jnp.where(sub == j + q, new[q], out)
        d = out
    return d


def invert_kernel(a_ref, o_ref, c_ref):
    size = a_ref.shape[0]
    o_ref[...] = a_ref[...]

    def step(k, carry):
        off = pl.multiple_of(k * BLOCK, BLOCK)
        pivot = block_inverse(o_ref[pl.ds(off, BLOCK), pl.ds(off, BLOCK)])
        c_ref[...] = o_ref[:, pl.ds(off, BLOCK)]
        o_ref[pl.ds(off, BLOCK), :] = nn(pivot, o_ref[pl.ds(off, BLOCK), :])
        o_ref[pl.ds(off, BLOCK), pl.ds(off, BLOCK)] = pivot
        pivot_rows = o_ref[pl.ds(off, BLOCK), :]
        for q in range(size // BLOCK):
            rows = slice(q * BLOCK, (q + 1) * BLOCK)

            @pl.when(k != q)
            def _():
                o_ref[rows, pl.ds(off, BLOCK)] = jnp.zeros((BLOCK, BLOCK), F32)
                o_ref[rows, :] = o_ref[rows, :] - nn(c_ref[rows, :], pivot_rows)

        return carry

    lax.fori_loop(0, size // BLOCK, step, 0)


def column_kernel(v_ref, inv_ref, diag_ref, z_ref, f_ref):
    z = nn(v_ref[0, 4], inv_ref[...])
    z_ref[...] = z
    f_ref[...] = jnp.concatenate([nt(diag_ref[1 + t], z) for t in range(3)], axis=1)


def panel_rows_of(ref, comp):
    return jnp.concatenate([ref[piece, 0, comp] for piece in range(ref.shape[0])], axis=1)


def root_inverse(g):
    n, nb = LIVE, 4
    lane = lax.broadcasted_iota(jnp.int32, (n, 128), 1)
    sub = lax.broadcasted_iota(jnp.int32, (n, 128), 0)
    e = jnp.concatenate([g, jnp.zeros((n, 128 - n), F32)], axis=1) + (lane == sub + n).astype(F32)
    for j in range(0, n, nb):
        m = [[None] * nb for _ in range(nb)]
        for r in range(nb):
            for c in range(r, nb):
                m[r][c] = jnp.broadcast_to(e[j + r : j + r + 1, j + c : j + c + 1], (8, 128))
        cols = [jnp.broadcast_to(e[:, j + q : j + q + 1], (n, 128)) for q in range(nb)]
        rows = [jnp.broadcast_to(e[j + q : j + q + 1, :], (8, 128)) for q in range(nb)]
        rec = []
        for q in range(nb):
            rec.append(1.0 / m[q][q])
            low = {r: m[q][r] * rec[q] for r in range(q + 1, nb)}
            for r in range(q + 1, nb):
                for c in range(r, nb):
                    m[r][c] = m[r][c] - low[r] * m[q][c]
                rows[r] = rows[r] - low[r] * rows[q]
                cols[r] = cols[r] - jnp.concatenate([low[r]] * (n // 8), axis=0) * cols[q]
        rows_n = [jnp.concatenate([t] * (n // 8), axis=0) for t in rows]
        out = e
        for q in range(nb):
            out = out - (cols[q] * jnp.concatenate([rec[q]] * (n // 8), axis=0)) * rows_n[q]
        out = jnp.where(sub >= j + nb, out, e)
        for q in range(nb):
            out = jnp.where(sub == j + q, rows_n[q], out)
        e = out
    d = jnp.sum(jnp.where(lane == sub, e, 0.0), axis=1, keepdims=True)
    return e[:, n : 2 * n] * (1.0 / jnp.sqrt(d))


def prepare_kernel(
    prank_ref, crank_ref, trank_ref, krank_ref,
    rows_ref, cols_ref, tr_ref, s_ref, inv_ref, zc_ref,
    zp_ref, w_ref, h_ref, k_ref, ri_ref, q_ref,
):
    tile = pl.program_id(0)
    r = s_ref.shape[0]
    zc = zc_ref[...]
    zp = nn(panel_rows_of(rows_ref, 4), inv_ref[...])
    zp_ref[0] = zp
    keep_p = lax.broadcasted_iota(jnp.int32, (r, r), 0) < prank_ref[tile]
    keep_c = lax.broadcasted_iota(jnp.int32, (r, r), 1) < crank_ref[0]
    keep = keep_p & keep_c
    w0 = jnp.where(keep, nt(panel_rows_of(rows_ref, 4), zc), 0.0)
    w_ref[0, 0] = w0
    for t in range(3):
        w_ref[0, 1 + t] = nt(panel_rows_of(rows_ref, 5 + t), zc) + nt(zp, cols_ref[0, 5 + t])
    live = (lax.broadcasted_iota(jnp.int32, (LIVE, s_ref.shape[1]), 0) < krank_ref[tile, 0]).astype(F32)
    s = s_ref[0:LIVE, :] * live
    keep_t = lax.broadcasted_iota(jnp.int32, (LIVE, r), 1) < trank_ref[tile, 0]
    for t in range(4):
        h_ref[0, t] = jnp.where(keep_t, nt(s, tr_ref[0, 0, 4 + t]), 0.0)
        k_ref[0, t] = nt(s, cols_ref[0, t])
    left = jnp.concatenate([h_ref[0, 0], -nt(k_ref[0, 0], w0)], axis=1)
    up = jnp.concatenate([tr_ref[0, 0, 0], panel_rows_of(rows_ref, 0)], axis=0)
    y = nn(left, up)
    sub = lax.broadcasted_iota(jnp.int32, (LIVE, LIVE), 0)
    lane = lax.broadcasted_iota(jnp.int32, (LIVE, LIVE), 1)
    g = nt(y, y) + ((sub == lane) & (sub >= krank_ref[tile, 0])).astype(F32)
    ri = root_inverse(g)
    ri_ref[0] = ri
    q_ref[0] = nn(ri, y)


def finish_kernel(
    prank_ref, crank_ref, trank_ref,
    rows_ref, cols_ref, tr_ref, f_ref, zp_ref, w_ref, h_ref, k_ref, ri_ref, q_ref,
    o_ref,
):
    tile = pl.program_id(0)
    r = h_ref.shape[3]
    width = q_ref.shape[2]
    keep_p = lax.broadcasted_iota(jnp.int32, (r, r), 0) < prank_ref[tile]
    keep_c = lax.broadcasted_iota(jnp.int32, (r, r), 1) < crank_ref[0]
    keep = keep_p & keep_c
    keep_t = lax.broadcasted_iota(jnp.int32, (LIVE, r), 1) < trank_ref[tile, 0]
    zf = nn(zp_ref[0], f_ref[...])
    w0 = w_ref[0, 0]
    dw = [jnp.where(keep, w_ref[0, 1 + t] - zf[:, t * r : (t + 1) * r], 0.0) for t in range(3)]
    ri = ri_ref[0]
    q = q_ref[0]
    h = [h_ref[0, t] for t in range(4)]
    k = [k_ref[0, t] for t in range(4)]
    left0 = nn(ri, jnp.concatenate([h[0], -nt(k[0], w0)], axis=1))
    left = [
        nn(ri, jnp.concatenate([h[1 + t], -(nt(k[1 + t], w0) + nt(k[0], dw[t]))], axis=1))
        for t in range(3)
    ]
    ups = [jnp.concatenate([tr_ref[0, 0, t], panel_rows_of(rows_ref, t)], axis=0) for t in range(4)]
    e = nn(jnp.concatenate(left, axis=0), ups[0])
    e = e + jnp.concatenate([nn(left0, ups[1 + t]) for t in range(3)], axis=0)
    m = nt(e, q)
    sub = lax.broadcasted_iota(jnp.int32, (LIVE, LIVE), 0)
    lane = lax.broadcasted_iota(jnp.int32, (LIVE, LIVE), 1)
    phi = []
    for t in range(3):
        mt = m[t * LIVE : (t + 1) * LIVE, :]
        mid = mt + mt.T
        phi.append(jnp.where(sub > lane, mid, jnp.where(sub == lane, 0.5 * mid, 0.0)))
    dq = e - nn(jnp.concatenate(phi, axis=0), q)
    qs = jnp.concatenate([q, dq], axis=0)
    js = nt(qs, ups[0])
    extra = [nt(q, ups[1 + t]) for t in range(3)]
    j0 = js[0:LIVE]
    j0u, j0p = jnp.where(keep_t, j0[:, :r], 0.0), j0[:, r:]
    n0 = jnp.concatenate([j0u, -nn(j0p, w0)], axis=1)
    ns = [n0]
    for t in range(3):
        jt = js[(1 + t) * LIVE : (2 + t) * LIVE] + extra[t]
        ns.append(
            jnp.concatenate(
                [jnp.where(keep_t, jt[:, :r], 0.0), -(nn(jt[:, r:], w0) + nn(j0p, dw[t]))], axis=1
            )
        )
    vs = [jnp.concatenate([tr_ref[0, 0, 4 + t], cols_ref[0, t]], axis=0) for t in range(4)]
    b = nn(jnp.concatenate(ns, axis=0), vs[0])
    up_scale = math.sqrt(width)
    down_scale = 1.0 / math.sqrt(r)
    zero = jnp.zeros((r - LIVE, width), F32)
    for t in range(4):
        o_ref[0, 0, t, 0:LIVE, :] = qs[t * LIVE : (t + 1) * LIVE] * up_scale
        bt = b[t * LIVE : (t + 1) * LIVE]
        if t:
            bt = bt + nn(n0, vs[t])
        o_ref[0, 0, 4 + t, 0:LIVE, :] = bt * down_scale
        o_ref[0, 0, t, LIVE:r, :] = zero
        o_ref[0, 0, 4 + t, LIVE:r, :] = zero


def whole(shape):
    return pl.BlockSpec(shape, lambda i: (0,) * len(shape))


def tiled(shape):
    return pl.BlockSpec(shape, lambda i: (i,) + (0,) * (len(shape) - 1))


def params():
    return pltpu.CompilerParams(vmem_limit_bytes=56 << 20)


def cost(flops, nbytes):
    return pl.CostEstimate(flops=int(flops), bytes_accessed=int(nbytes), transcendentals=0)


def on_device(
    diag, panel_rows, panel_cols, trailing, sketch, panel_rank, col_rank, tile_rank, keep_rank
):
    rank, width = sketch.shape
    tiles = trailing.shape[0]
    pieces = lax.axis_size("col")
    a = lax.all_gather(diag[0], "row", axis=0, tiled=True)
    a, panel_rows, panel_cols = lax.optimization_barrier((a, panel_rows, panel_cols))
    cols = lax.all_gather(panel_cols, "row", axis=2, tiled=True)
    rows = lax.all_gather(panel_rows, "col", axis=0, tiled=False)
    inverse = pl.pallas_call(
        invert_kernel,
        out_shape=jax.ShapeDtypeStruct((width, width), F32),
        scratch_shapes=[pltpu.VMEM((width, BLOCK), F32)],
        compiler_params=params(),
        cost_estimate=cost(60e9, 8 << 20),
        name="invert",
    )(a)
    zc, f = pl.pallas_call(
        column_kernel,
        out_shape=(
            jax.ShapeDtypeStruct((rank, width), F32),
            jax.ShapeDtypeStruct((diag.shape[1], 3 * rank), F32),
        ),
        compiler_params=params(),
        cost_estimate=cost(2e9, 6 << 20),
        name="columns",
    )(cols, inverse, diag)
    f_all = lax.all_gather(f, "row", axis=0, tiled=True)
    smem = pl.BlockSpec(memory_space=pltpu.SMEM)
    rows_spec = pl.BlockSpec((pieces, 1) + rows.shape[2:], lambda i: (0, i, 0, 0, 0))
    tr_spec = tiled((1,) + trailing.shape[1:])
    mids = dict(
        zp=(tiles, rank, width),
        w=(tiles, 4, rank, rank),
        h=(tiles, 4, LIVE, rank),
        k=(tiles, 4, LIVE, rank),
        ri=(tiles, LIVE, LIVE),
        q=(tiles, LIVE, width),
    )
    mid_specs = [tiled((1,) + s[1:]) for s in mids.values()]
    mid = pl.pallas_call(
        prepare_kernel,
        grid=(tiles,),
        in_specs=[smem] * 4
        + [rows_spec, whole(cols.shape), tr_spec, whole(sketch.shape), whole(inverse.shape), whole(zc.shape)],
        out_specs=mid_specs,
        out_shape=[jax.ShapeDtypeStruct(s, F32) for s in mids.values()],
        compiler_params=params(),
        cost_estimate=cost(10e9, 20 << 20),
        name="prepare",
    )(panel_rank, col_rank, tile_rank, keep_rank, rows, cols, trailing, sketch, inverse, zc)
    return pl.pallas_call(
        finish_kernel,
        grid=(tiles,),
        in_specs=[smem] * 3
        + [rows_spec, whole(cols.shape), tr_spec, whole(f_all.shape)]
        + mid_specs,
        out_specs=tr_spec,
        out_shape=jax.ShapeDtypeStruct(trailing.shape, F32),
        compiler_params=params(),
        cost_estimate=cost(10e9, 20 << 20),
        name="finish",
    )(panel_rank, col_rank, tile_rank, rows, cols, trailing, f_all, *mid)


def solution(mesh):
    in_specs = (
        P(None, "row", None),
        P("row", None, None, "col"),
        P("col", None, "row", None),
        P("row", "col", None, None, None),
        P(),
        P("row"),
        P("col"),
        P("row", "col"),
        P("row", "col"),
    )
    out_specs = P("row", "col", None, None, None)
    return jax.shard_map(
        on_device, mesh=mesh, in_specs=in_specs, out_specs=out_specs, check_vma=False
    )
```

time: 744 us -> 238 us (0.32); the launches traced: 734 us -> 238 us
  other arithmetic: 299 us -> 0 us
  matrix products: 152 us -> 0 us
  Pallas kernels: 0 us -> 130 us
  waiting for transfers between devices: 163 us -> 57.7 us
  local copies, waits for them, and re-layouts: 98.7 us -> 9.79 us
  blocking collectives: 0 us -> 26.8 us
    another operation x40 -> x0, other arithmetic: 280 us -> none  [the longest x30 172 us: on_device(): lower_factor = jnp.linalg.cholesky(primal)]
    pallas_call x0 -> x4, Pallas kernels: none -> 130 us  [the longest x1 78.3 us: on_device(): pl.pallas_call(invert_kernel, out_shape=jax.ShapeDtypeStruct((width, widt...]
    all_gather x3, waiting for transfers between devices: 163 us -> 57 us  [the longest x1 57 us: on_device(): a = lax.all_gather(diag[0], 'row', axis=0, tiled=True)]
    dot_general x49 -> x0, matrix products: 89.6 us -> none  [the longest x48 69.4 us: highest_accuracy(): jnp.dot(left, right, precision=HIGHEST_PRECISION, preferred_element_type=...]
    another operation x78 -> x0, matrix products: 62.6 us -> none  [the longest x14 22.9 us: on_device(): lower_factor = jnp.linalg.cholesky(primal)]
    another operation x45 -> x0, local copies, waits for them, and re-layouts: 34.6 us -> none
    all_gather x0 -> x1, blocking collectives: none -> 26.8 us  [on_device(): f_all = lax.all_gather(f, 'row', axis=0, tiled=True)]
    slice x5 -> x1, local copies, waits for them, and re-layouts: 24.5 us -> 1.57 us  [on_device(): a = lax.all_gather(diag[0], 'row', axis=0, tiled=True)]
  transfers between devices with their start and end apart: 3 -> 3, of which waited for: 3 -> 1; matrix products, arithmetic and copies ran while one was open for 4% -> 3% of each run, Pallas kernels for 0% -> 36%
where the time goes in v1:
time: 238 us
  Pallas kernels  130 us (55%)
  waiting for transfers between devices  57.7 us (24%)
  blocking collectives  26.8 us (11%)
  between operations  13.8 us (6%)
  local copies, waits for them, and re-layouts  9.79 us (4%)
    pallas_call x1, Pallas kernels, on_device(): pl.pallas_call(invert_kernel, out_shape=jax.ShapeDtypeStruct((width, widt...  78.3 us
    all_gather x1, waiting for transfers between devices, on_device(): a = lax.all_gather(diag[0], 'row', axis=0, tiled=True)  57 us
    all_gather x1, blocking collectives, on_device(): f_all = lax.all_gather(f, 'row', axis=0, tiled=True)  26.8 us
    pallas_call x1, Pallas kernels, on_device(): pl.pallas_call(finish_kernel, grid=(tiles,), in_specs=[smem] * 3 + [rows_...  24.5 us
    pallas_call x1, Pallas kernels, on_device(): pl.pallas_call(prepare_kernel, grid=(tiles,), in_specs=[smem] * 4 + [rows...  20.5 us
    pallas_call x1, Pallas kernels, on_device(): pl.pallas_call(column_kernel, out_shape=(jax.ShapeDtypeStruct((rank, widt...  6.78 us
  transfers between devices with their start and end apart: 3, of which 1 were waited for; matrix products, arithmetic and copies ran while one was open for 3% of the time, Pallas kernels for 36%

profile of v1, /device:TPU:1, one launch (start us, length us, event | category | flops | bytes accessed | tf_op | source)
XLA Modules:
  0.0 238.2 jit_solution(4344715583930761609)
XLA Ops:
  6.5 0.0 all-gather.8.cloned.1.call-start
  6.5 1.6 slice.3
  8.1 0.0 all-gather.8.cloned.1.call-update
  8.1 0.0 all-gather.6.cloned.1.call-start
  8.2 57.0 %all-gather.8.cloned.1.call-done = f32[1,1024,1024]{2,1,0:T(8,128)} async-done(((f32[1,32,1024]{2,1,0:T(8,128)}), f32[1,1024,1024]{2,1,0:T(8,128)}) %all-gather.8.cloned.1.call-update) | async-done | bytes 4194320 | tf_op jit(solution)/shard_map/all_gather | solution.py:283
  65.1 1.5 copy.13
  66.6 0.0 all-gather.6.cloned.1.call-update
  66.6 0.0 all-gather.10.cloned.1.call-start
  66.7 0.7 all-gather.10.cloned.1.call-update
  67.4 1.3 copy.18.trank_ref
  69.3 1.3 copy.16.krank_ref
  70.6 78.3 %invert.1.inv_ref = f32[1024,1024]{1,0:T(8,128)} custom-call(f32[1024,1024]{1,0:T(8,128)} %bitcast.4), custom_call_target="tpu_custom_call" | custom-call | flops 60000002048 | bytes 8388608 | tf_op jit(solution)/shard_map/invert/pallas_call | solution.py:287
  148.9 0.0 all-gather.6.cloned.1.call-done
  148.9 4.2 %copy.19.v_ref.cols_ref = f32[1,8,64,1024]{3,2,1,0:T(8,128)} copy(f32[1,8,64,1024]{3,1,0,2:T(8,128)} %all-gather.6.cloned.1.call-done) | data formatting | bytes 4194304 | tf_op jit(solution)/shard_map/all_gather | solution.py:285
  153.0 6.8 %columns.1 = (f32[64,1024]{1,0:T(8,128)}, f32[32,192]{1,0:T(8,128)}) custom-call(f32[1,8,64,1024]{3,2,1,0:T(8,128)} %copy.19.v_ref.cols_ref, f32[1024,1024]{1,0:T(8,128)} %invert.1.inv_ref, f32[4,32,1024]{2,1,0:T(8,128)} %diag_ref.1), custom_call_target="tpu_custom_call" | custom-call | flops 2000000000 | bytes 6291456 | tf_op jit(solution)/shard_map/columns/pallas_call | solution.py:295
  159.8 26.8 %all_gather.19.f_ref = f32[1024,192]{1,0:T(8,128)} all-gather(f32[32,192]{1,0:T(8,128)} %get-tuple-element.19), channel_id=1, replica_groups=mesh['row'=32,'col'=8] {'row'}, dimensions={0}, use_global_device_ids=true | all-gather | bytes 811008 | tf_op jit(solution)/shard_map/all_gather | solution.py:305
  186.6 0.0 all-gather.10.cloned.1.call-done
  186.6 20.5 %prepare.1 = (f32[2,64,1024]{2,1,0:T(8,128)}, f32[2,4,64,64]{3,2,1,0:T(8,128)}, f32[2,4,32,64]{3,2,1,0:T(8,128)}, f32[2,4,32,64]{3,2,1,0:T(8,128)}, f32[2,32,32]{2,1,0:T(8,128)}, /*index=5*/f32[2,32,1024]{2,1,0:T(8,128)}) custom-call(s32[2]{0:T(128)} %prank_ref.3, s32[1]{0:T(128)S(6)} %copy.20.crank_ref, s32[2,1]{1,0:T(2,128)} %copy.18.trank_ref, ...), custom_call_target="tpu_custom_call" | custom-call | flops 10000000000 | bytes 20971520 | tf_op jit(solution)/shard_map/prepare/pallas_call | solution.py:318
  207.1 24.5 %finish.1 = f32[2,1,8,64,1024]{4,3,2,1,0:T(8,128)} custom-call(s32[2]{0:T(128)} %prank_ref.3, s32[1]{0:T(128)S(6)} %copy.20.crank_ref, s32[2,1]{1,0:T(2,128)} %copy.18.trank_ref, f32[8,2,8,64,128]{4,3,2,1,0:T(8,128)} %bitcast.3, f32[1,8,64,1024]{3,2,1,0:T(8,128)} %copy.19.v_ref.cols_ref, f32[2,1,8,64,1024]{4,3,2,1,0:T(8,128)} %tr_ref.3, ...), custom_call_target="tpu_custom_call" | custom-call | flops 10000000000 | bytes 20971520 | tf_op jit(solution)/shard_map/finish/pallas_call | solution.py:329
Async XLA Ops:
  6.5 58.6 %all-gather.8.cloned.1.call-start = ((), (), s32[]{:S(2)}) async-start(), calls=%async_computation.1 | async-start | bytes 4325376 | tf_op jit(solution)/shard_map/all_gather | solution.py:283
  8.1 140.7 %all-gather.6.cloned.1.call-start = ((), (), s32[]{:S(2)}) async-start(), calls=%async_computation | async-start | bytes 2162688 | tf_op jit(solution)/shard_map/all_gather | solution.py:285
  66.6 120.0 %all-gather.10.cloned.1.call-start = ((), (), s32[]{:S(2)}) async-start(), calls=%async_computation.2 | async-start | bytes 4718592 | tf_op jit(solution)/shard_map/all_gather | solution.py:286
Sparse Core Ops, SparseCore 0:
  9.9 55.2 all-gather.7
  67.7 48.2 all-gather.5
  117.8 53.7 all-gather.9

commit v2 on v1

--- a/solution.py
+++ b/solution.py
@@ -13,6 +13,10 @@
 NPIV = 8
 LIVE = 32
 F32 = jnp.float32
+BF16 = jnp.bfloat16
+MESH = pl.DeviceIdType.MESH
+SIDE = 4
+SENDS = 4 * SIDE + 2 * SIDE + SIDE * SIDE - SIDE + 2 + 2 + 2
 
 
 def nn(x, y):
@@ -63,7 +67,28 @@
     return [t[i] + o[i] for i in range(h)] + [[o[j][i] for j in range(h)] + g[i] for i in range(h)]
 
 
-def block_inverse(d):
+def split3(x):
+    a = x.astype(BF16)
+    r = x - a.astype(F32)
+    b = r.astype(BF16)
+    return a, b, (r - b.astype(F32)).astype(BF16)
+
+
+def left6(parts):
+    a, b, c = parts
+    return jnp.concatenate([a, b, a, b, a, c], axis=1)
+
+
+def right6(parts):
+    a, b, c = parts
+    return jnp.concatenate([a, a, b, b, c, a], axis=0)
+
+
+def mm(x, y):
+    return lax.dot_general(x, y, (((1,), (0,)), ((), ())), preferred_element_type=F32)
+
+
+def pivot_steps(d):
     n = d.shape[0]
     lane = lax.broadcasted_iota(jnp.int32, (n, n), 1)
     sub = lax.broadcasted_iota(jnp.int32, (n, n), 0)
@@ -89,35 +114,212 @@
         for q in range(NPIV):
             out = jnp.where(sub == j + q, new[q], out)
         d = out
-    return d
-
-
-def invert_kernel(a_ref, o_ref, c_ref):
-    size = a_ref.shape[0]
-    o_ref[...] = a_ref[...]
-
-    def step(k, carry):
+        yield d
+
+
+def invert_kernel(g_ref, o_ref, p_ref, l_ref, r_ref):
+    size = o_ref.shape[0]
+    blocks = size // BLOCK
+    share = size // g_ref.shape[0]
+    for i in range(g_ref.shape[0]):
+        o_ref[i * share : (i + 1) * share, :] = g_ref[i, 0:share, :]
+    d = None
+    for d in pivot_steps(o_ref[0:BLOCK, 0:BLOCK]):
+        pass
+    p_ref[...] = d
+
+    def step(k, last):
         off = pl.multiple_of(k * BLOCK, BLOCK)
-        pivot = block_inverse(o_ref[pl.ds(off, BLOCK), pl.ds(off, BLOCK)])
-        c_ref[...] = o_ref[:, pl.ds(off, BLOCK)]
-        o_ref[pl.ds(off, BLOCK), :] = nn(pivot, o_ref[pl.ds(off, BLOCK), :])
-        o_ref[pl.ds(off, BLOCK), pl.ds(off, BLOCK)] = pivot
-        pivot_rows = o_ref[pl.ds(off, BLOCK), :]
-        for q in range(size // BLOCK):
-            rows = slice(q * BLOCK, (q + 1) * BLOCK)
-
-            @pl.when(k != q)
-            def _():
-                o_ref[rows, pl.ds(off, BLOCK)] = jnp.zeros((BLOCK, BLOCK), F32)
-                o_ref[rows, :] = o_ref[rows, :] - nn(c_ref[rows, :], pivot_rows)
-
+        here = pl.ds(off, BLOCK)
+        p = p_ref[...]
+        p6 = left6(split3(p))
+        for q, part in enumerate(split3(o_ref[:, here])):
+            l_ref[:, q * BLOCK : (q + 1) * BLOCK] = part
+
+        def left_of(row):
+            return left6([l_ref[pl.ds(row, BLOCK), q * BLOCK : (q + 1) * BLOCK] for q in range(3)])
+
+        steps, found = iter(()), None
+        if not last:
+            nxt = pl.multiple_of((k + 1) * BLOCK, BLOCK)
+            rn = mm(p6, right6(split3(o_ref[here, pl.ds(nxt, BLOCK)])))
+            steps = pivot_steps(
+                o_ref[pl.ds(nxt, BLOCK), pl.ds(nxt, BLOCK)] - mm(left_of(nxt), right6(split3(rn)))
+            )
+        o_ref[here, here] = jnp.zeros((BLOCK, BLOCK), F32)
+        for h in range(2):
+            cs = slice(h * size // 2, (h + 1) * size // 2)
+            o_ref[here, cs] = mm(p6, right6(split3(o_ref[here, cs])))
+        o_ref[here, here] = p
+        for q, part in enumerate(split3(o_ref[here, :])):
+            r_ref[q * BLOCK : (q + 1) * BLOCK, :] = part
+        for q in range(1, blocks):
+            row = pl.multiple_of(lax.rem(k + q, blocks) * BLOCK, BLOCK)
+            o_ref[pl.ds(row, BLOCK), here] = jnp.zeros((BLOCK, BLOCK), F32)
+            left = left_of(row)
+            for h in range(2):
+                cs = slice(h * size // 2, (h + 1) * size // 2)
+                right = right6([r_ref[q3 * BLOCK : (q3 + 1) * BLOCK, cs] for q3 in range(3)])
+                o_ref[pl.ds(row, BLOCK), cs] = o_ref[pl.ds(row, BLOCK), cs] - mm(left, right)
+                found = next(steps, found)
+        for found in steps:
+            pass
+        if not last:
+            p_ref[...] = found
+
+    def body(k, carry):
+        step(k, False)
         return carry
 
-    lax.fori_loop(0, size // BLOCK, step, 0)
-
-
-def column_kernel(v_ref, inv_ref, diag_ref, z_ref, f_ref):
-    z = nn(v_ref[0, 4], inv_ref[...])
+    lax.fori_loop(0, blocks - 1, body, 0)
+    step(blocks - 1, True)
+
+
+def gather_kernel(x_ref, o_ref, stage_ref, local_sem, send_sem, recv_sem, pair_sem):
+    row = lax.axis_index("row")
+    col = lax.axis_index("col")
+    core = lax.rem(row, 2)
+    x0 = lax.rem(row // 2, SIDE)
+    y0 = row // (2 * SIDE)
+    half = x_ref.shape[0] // 2
+
+    def device(i1, i2, c=None):
+        c = core if c is None else c
+        dx = i1 * (1 - core) + i2 * core
+        dy = i1 * core + i2 * (1 - core)
+        return (lax.rem(y0 + dy + SIDE, SIDE) * SIDE + lax.rem(x0 + dx + SIDE, SIDE)) * 2 + c
+
+    peers = {
+        "a+": device(1, 0),
+        "a-": device(-1, 0),
+        "b+": device(0, 1),
+        "b-": device(0, -1),
+        "pair": device(0, 0, 1 - core),
+    }
+    shift = {"a+": (1, 0), "a-": (-1, 0), "b+": (0, 1), "b-": (0, -1)}
+    barrier = pltpu.get_barrier_semaphore()
+    for to in peers.values():
+        pl.semaphore_signal(barrier, inc=1, device_id=(to, col), device_id_type=MESH)
+    pl.semaphore_wait(barrier, len(peers))
+
+    mine = pltpu.make_async_copy(x_ref, stage_ref, local_sem.at[0])
+    mine.start()
+    sent = []
+
+    def part(ref, h):
+        return ref if h is None else ref.at[pl.ds(h * half, half)]
+
+    def send(i1, i2, to, h=None):
+        owner = device(i1, i2)
+        source = x_ref if (i1, i2) == (0, 0) else o_ref.at[owner]
+        if to == "pair":
+            sem = pair_sem.at[i1 % SIDE, i2 % SIDE]
+        else:
+            s1, s2 = shift[to]
+            sem = recv_sem.at[(i1 - s1) % SIDE, (i2 - s2) % SIDE, h or 0]
+        copy = pltpu.make_async_remote_copy(
+            src_ref=part(source, h),
+            dst_ref=part(o_ref.at[owner], h),
+            send_sem=send_sem.at[len(sent)],
+            recv_sem=sem,
+            device_id=(peers[to], col),
+            device_id_type=MESH,
+        )
+        copy.start()
+        sent.append(copy)
+
+    def arrive(i1, i2, h=None, pair=False):
+        owner = device(i1, i2)
+        sem = pair_sem.at[i1 % SIDE, i2 % SIDE] if pair else recv_sem.at[i1 % SIDE, i2 % SIDE, h or 0]
+        dst = part(o_ref.at[owner], h)
+        pltpu.make_async_remote_copy(
+            src_ref=dst,
+            dst_ref=dst,
+            send_sem=send_sem.at[0],
+            recv_sem=sem,
+            device_id=(peers["pair"], col),
+            device_id_type=MESH,
+        ).wait_recv()
+
+    def spread(i1):
+        send(i1, 0, "b+")
+        send(i1, 0, "b-")
+        send(i1, 0, "pair")
+
+    send(0, 0, "a+")
+    send(0, 0, "a-")
+    spread(0)
+    mine.wait()
+    keep = pltpu.make_async_copy(stage_ref, o_ref.at[row], local_sem.at[1])
+    keep.start()
+    arrive(-1, 0)
+    send(-1, 0, "a+", 0)
+    spread(-1)
+    arrive(1, 0)
+    send(1, 0, "a-", 1)
+    spread(1)
+    arrive(2, 0, 0)
+    arrive(2, 0, 1)
+    spread(2)
+    order = (0, -1, 1, 2)
+    for i1 in order:
+        arrive(i1, -1)
+        send(i1, -1, "b+", 0)
+        send(i1, -1, "pair")
+        arrive(i1, 1)
+        send(i1, 1, "b-", 1)
+        send(i1, 1, "pair")
+    for i1 in order:
+        arrive(i1, 2, 0)
+        arrive(i1, 2, 1)
+        send(i1, 2, "pair")
+    for i1 in range(SIDE):
+        for i2 in range(SIDE):
+            arrive_pair(o_ref, device, pair_sem, send_sem, i1, i2, core, peers["pair"], col)
+    for copy in sent:
+        copy.wait_send()
+    keep.wait()
+
+
+def arrive_pair(o_ref, device, pair_sem, send_sem, i1, i2, core, pair, col):
+    owner = device(i2, i1, 1 - core)
+    pltpu.make_async_remote_copy(
+        src_ref=o_ref.at[owner],
+        dst_ref=o_ref.at[owner],
+        send_sem=send_sem.at[0],
+        recv_sem=pair_sem.at[i1, i2],
+        device_id=(pair, col),
+        device_id_type=MESH,
+    ).wait_recv()
+
+
+def gather(block, collective_id):
+    devices = lax.axis_size("row")
+    return pl.pallas_call(
+        gather_kernel,
+        out_shape=jax.ShapeDtypeStruct((devices,) + block.shape, F32),
+        in_specs=[pl.BlockSpec(memory_space=pl.ANY)],
+        out_specs=pl.BlockSpec(memory_space=pl.ANY),
+        scratch_shapes=[
+            pltpu.VMEM(block.shape, F32),
+            pltpu.SemaphoreType.DMA((2,)),
+            pltpu.SemaphoreType.DMA((SENDS,)),
+            pltpu.SemaphoreType.DMA((SIDE, SIDE, 2)),
+            pltpu.SemaphoreType.DMA((SIDE, SIDE)),
+        ],
+        compiler_params=pltpu.CompilerParams(collective_id=collective_id, has_side_effects=True),
+        cost_estimate=cost(0, 12 << 20),
+        name="gather",
+    )(block)
+
+
+def column_kernel(g_ref, inv_ref, diag_ref, z_ref, f_ref, c_ref):
+    devices, extent, width = g_ref.shape
+    share = width // devices
+    for i in range(devices):
+        for j in range((extent - share) // 8):
+            c_ref[:, i * ((extent - share) // 8) + j, :] = g_ref[i, share + 8 * j : share + 8 * (j + 1), :]
+    z = nn(c_ref[4], inv_ref[...])
     z_ref[...] = z
     f_ref[...] = jnp.concatenate([nt(diag_ref[1 + t], z) for t in range(3)], axis=1)
 
@@ -175,13 +377,13 @@
     w0 = jnp.where(keep, nt(panel_rows_of(rows_ref, 4), zc), 0.0)
     w_ref[0, 0] = w0
     for t in range(3):
-        w_ref[0, 1 + t] = nt(panel_rows_of(rows_ref, 5 + t), zc) + nt(zp, cols_ref[0, 5 + t])
+        w_ref[0, 1 + t] = nt(panel_rows_of(rows_ref, 5 + t), zc) + nt(zp, cols_ref[5 + t])
     live = (lax.broadcasted_iota(jnp.int32, (LIVE, s_ref.shape[1]), 0) < krank_ref[tile, 0]).astype(F32)
     s = s_ref[0:LIVE, :] * live
     keep_t = lax.broadcasted_iota(jnp.int32, (LIVE, r), 1) < trank_ref[tile, 0]
     for t in range(4):
         h_ref[0, t] = jnp.where(keep_t, nt(s, tr_ref[0, 0, 4 + t]), 0.0)
-        k_ref[0, t] = nt(s, cols_ref[0, t])
+        k_ref[0, t] = nt(s, cols_ref[t])
     left = jnp.concatenate([h_ref[0, 0], -nt(k_ref[0, 0], w0)], axis=1)
     up = jnp.concatenate([tr_ref[0, 0, 0], panel_rows_of(rows_ref, 0)], axis=0)
     y = nn(left, up)
@@ -243,7 +445,7 @@
                 [jnp.where(keep_t, jt[:, :r], 0.0), -(nn(jt[:, r:], w0) + nn(j0p, dw[t]))], axis=1
             )
         )
-    vs = [jnp.concatenate([tr_ref[0, 0, 4 + t], cols_ref[0, t]], axis=0) for t in range(4)]
+    vs = [jnp.concatenate([tr_ref[0, 0, 4 + t], cols_ref[t]], axis=0) for t in range(4)]
     b = nn(jnp.concatenate(ns, axis=0), vs[0])
     up_scale = math.sqrt(width)
     down_scale = 1.0 / math.sqrt(r)
@@ -280,29 +482,33 @@
     rank, width = sketch.shape
     tiles = trailing.shape[0]
     pieces = lax.axis_size("col")
-    a = lax.all_gather(diag[0], "row", axis=0, tiled=True)
-    a, panel_rows, panel_cols = lax.optimization_barrier((a, panel_rows, panel_cols))
-    cols = lax.all_gather(panel_cols, "row", axis=2, tiled=True)
     rows = lax.all_gather(panel_rows, "col", axis=0, tiled=False)
+    own_cols = panel_cols[0].transpose(1, 0, 2).reshape(-1, width)
+    gathered = gather(jnp.concatenate([diag[0], own_cols], axis=0), 1)
     inverse = pl.pallas_call(
         invert_kernel,
         out_shape=jax.ShapeDtypeStruct((width, width), F32),
-        scratch_shapes=[pltpu.VMEM((width, BLOCK), F32)],
+        scratch_shapes=[
+            pltpu.VMEM((BLOCK, BLOCK), F32),
+            pltpu.VMEM((width, 3 * BLOCK), BF16),
+            pltpu.VMEM((3 * BLOCK, width), BF16),
+        ],
         compiler_params=params(),
         cost_estimate=cost(60e9, 8 << 20),
         name="invert",
-    )(a)
-    zc, f = pl.pallas_call(
+    )(gathered)
+    zc, f, cols = pl.pallas_call(
         column_kernel,
         out_shape=(
             jax.ShapeDtypeStruct((rank, width), F32),
             jax.ShapeDtypeStruct((diag.shape[1], 3 * rank), F32),
+            jax.ShapeDtypeStruct((panel_cols.shape[1], rank, width), F32),
         ),
         compiler_params=params(),
         cost_estimate=cost(2e9, 6 << 20),
         name="columns",
-    )(cols, inverse, diag)
-    f_all = lax.all_gather(f, "row", axis=0, tiled=True)
+    )(gathered, inverse, diag)
+    f_all = gather(f, 2).reshape(width, 3 * rank)
     smem = pl.BlockSpec(memory_space=pltpu.SMEM)
     rows_spec = pl.BlockSpec((pieces, 1) + rows.shape[2:], lambda i: (0, i, 0, 0, 0))
     tr_spec = tiled((1,) + trailing.shape[1:])

time: 238 us -> 183 us (0.77)
  waiting for transfers between devices: 57.7 us -> 0.73 us
  Pallas kernels: 130 us -> 164 us
  blocking collectives: 26.8 us -> 0 us
  local copies, waits for them, and re-layouts: 9.79 us -> 3.08 us
    all_gather x2 -> x0, waiting for transfers between devices: 57 us -> none  [the longest x1 57 us: on_device(): a = lax.all_gather(diag[0], 'row', axis=0, tiled=True)]
    pallas_call x0 -> x2, Pallas kernels: none -> 46.4 us  [gather(): pl.pallas_call(gather_kernel, out_shape=jax.ShapeDtypeStruct((devices,) +...]
    all_gather x1 -> x0, blocking collectives: 26.8 us -> none  [on_device(): f_all = lax.all_gather(f, 'row', axis=0, tiled=True)]
    pallas_call x1, Pallas kernels: 78.3 us -> 63.1 us  [on_device(): pl.pallas_call(invert_kernel, out_shape=jax.ShapeDtypeStruct((width, widt...]
    all_gather x1 -> x0, local copies, waits for them, and re-layouts: 4.18 us -> none  [on_device(): cols = lax.all_gather(panel_cols, 'row', axis=2, tiled=True)]
    pallas_call x1, Pallas kernels: 6.78 us -> 9.18 us  [on_device(): pl.pallas_call(column_kernel, out_shape=(jax.ShapeDtypeStruct((rank, widt...]
  transfers between devices with their start and end apart: 3 -> 1, of which waited for: 1 -> 0; matrix products, arithmetic and copies ran while one was open for 3% -> 2% of each run, Pallas kernels for 36% -> 65%
where the time goes in v2:
time: 183 us
  Pallas kernels  164 us (90%)
  between operations  14.1 us (8%)
  local copies, waits for them, and re-layouts  3.08 us (2%)
    pallas_call x1, Pallas kernels, on_device(): pl.pallas_call(invert_kernel, out_shape=jax.ShapeDtypeStruct((width, widt...  63.1 us
    pallas_call x2, Pallas kernels, gather(): pl.pallas_call(gather_kernel, out_shape=jax.ShapeDtypeStruct((devices,) +...  46.4 us
    pallas_call x1, Pallas kernels, on_device(): pl.pallas_call(finish_kernel, grid=(tiles,), in_specs=[smem] * 3 + [rows_...  24.6 us
    pallas_call x1, Pallas kernels, on_device(): pl.pallas_call(prepare_kernel, grid=(tiles,), in_specs=[smem] * 4 + [rows...  20.7 us
    pallas_call x1, Pallas kernels, on_device(): pl.pallas_call(column_kernel, out_shape=(jax.ShapeDtypeStruct((rank, widt...  9.18 us
  transfers between devices with their start and end apart: 1, of which 0 were waited for; matrix products, arithmetic and copies ran while one was open for 2% of the time, Pallas kernels for 65%

profile of v2, /device:TPU:1, one launch (start us, length us, event | category | flops | bytes accessed | tf_op | source)
XLA Modules:
  0.0 182.6 jit_solution(5937778848367953258)
XLA Ops:
  6.5 0.0 copy-start
  6.5 0.0 copy-start.1
  6.5 0.0 all-gather.3.cloned.1.call-start
  6.5 0.7 all-gather.3.cloned.1.call-update
  7.3 0.9 copy.19
  8.1 0.9 slice_bitcast_fusion
  9.0 0.7 pad_maximum_fusion.x_ref
  9.7 28.6 %gather.2.g_ref = f32[32,48,1024]{2,1,0:T(8,128)} custom-call(f32[48,1024]{1,0:T(8,128)} %pad_maximum_fusion.x_ref), custom_call_target="tpu_custom_call" | custom-call | bytes 12582912 | tf_op jit(solution)/shard_map/gather/pallas_call | solution.py:298
  38.4 0.0 copy-done
  38.4 0.7 copy.17.trank_ref
  39.7 0.0 copy-done.1
  39.7 0.6 copy.16.krank_ref
  40.3 63.1 %invert.1.inv_ref = f32[1024,1024]{1,0:T(8,128)} custom-call(f32[32,48,1024]{2,1,0:T(8,128)} %gather.2.g_ref), custom_call_target="tpu_custom_call" | custom-call | flops 60000002048 | bytes 8388608 | tf_op jit(solution)/shard_map/invert/pallas_call | solution.py:488
  103.4 9.2 %columns.1 = (f32[64,1024]{1,0:T(8,128)}, f32[32,192]{1,0:T(8,128)}, f32[8,64,1024]{2,1,0:T(8,128)}) custom-call(f32[32,48,1024]{2,1,0:T(8,128)} %gather.2.g_ref, f32[1024,1024]{1,0:T(8,128)} %invert.1.inv_ref, f32[4,32,1024]{2,1,0:T(8,128)} %diag_ref.1), custom_call_target="tpu_custom_call" | custom-call | flops 2000000000 | bytes 6291456 | tf_op jit(solution)/shard_map/columns/pallas_call | solution.py:500
  112.6 17.8 %gather.3 = f32[32,32,192]{2,1,0:T(8,128)} custom-call(f32[32,192]{1,0:T(8,128)} %get-tuple-element.15.x_ref), custom_call_target="tpu_custom_call" | custom-call | bytes 12582912 | tf_op jit(solution)/shard_map/gather/pallas_call | solution.py:298
  130.4 0.0 all-gather.3.cloned.1.call-done
  130.4 20.7 %prepare.1 = (f32[2,64,1024]{2,1,0:T(8,128)}, f32[2,4,64,64]{3,2,1,0:T(8,128)}, f32[2,4,32,64]{3,2,1,0:T(8,128)}, f32[2,4,32,64]{3,2,1,0:T(8,128)}, f32[2,32,32]{2,1,0:T(8,128)}, /*index=5*/f32[2,32,1024]{2,1,0:T(8,128)}) custom-call(s32[2]{0:T(128)} %prank_ref.3, s32[1]{0:T(128)S(6)} %copy.20.crank_ref, s32[2,1]{1,0:T(2,128)} %copy.17.trank_ref, ...), custom_call_target="tpu_custom_call" | custom-call | flops 10000000000 | bytes 20971520 | tf_op jit(solution)/shard_map/prepare/pallas_call | solution.py:524
  151.1 24.6 %finish.1 = f32[2,1,8,64,1024]{4,3,2,1,0:T(8,128)} custom-call(s32[2]{0:T(128)} %prank_ref.3, s32[1]{0:T(128)S(6)} %copy.20.crank_ref, s32[2,1]{1,0:T(2,128)} %copy.17.trank_ref, f32[8,2,8,64,128]{4,3,2,1,0:T(8,128)} %bitcast.14, f32[8,64,1024]{2,1,0:T(8,128)} %get-tuple-element.14.cols_ref, f32[2,1,8,64,1024]{4,3,2,1,0:T(8,128)} %tr_ref.3, ...), custom_call_target="tpu_custom_call" | custom-call | flops 10000000000 | bytes 20971520 | tf_op jit(solution)/shard_map/finish/pallas_call | solution.py:535
Async XLA Ops:
  6.5 31.8 %copy-start = (s32[2,1]{0,1:T(1,128)S(1)}, s32[2,1]{0,1:T(1,128)}, u32[]{:S(2)}) copy-start(s32[2,1]{0,1:T(1,128)} %param.16) | copy-start | bytes 28
  6.5 33.2 %copy-start.1 = (s32[2,1]{0,1:T(1,128)S(1)}, s32[2,1]{0,1:T(1,128)}, u32[]{:S(2)}) copy-start(s32[2,1]{0,1:T(1,128)} %param.17) | copy-start | bytes 28
  6.5 123.9 %all-gather.3.cloned.1.call-start = ((), (), s32[]{:S(2)}) async-start(), calls=%async_computation | async-start | bytes 4718592 | tf_op jit(solution)/shard_map/all_gather | solution.py:485
Sparse Core Ops, SparseCore 0:
  9.1 58.3 all-gather.2

commit v3 on v2

--- a/solution.py
+++ b/solution.py
@@ -86,6 +86,40 @@
 
 def mm(x, y):
     return lax.dot_general(x, y, (((1,), (0,)), ((), ())), preferred_element_type=F32)
+
+
+def split2(x):
+    a = x.astype(BF16)
+    return a, (x - a.astype(F32)).astype(BF16)
+
+
+def nn2(x, y):
+    m = x.shape[0]
+    a, b = split2(x)
+    left = jnp.concatenate([jnp.concatenate([a, a], axis=1), jnp.concatenate([b, b], axis=1)], axis=0)
+    r = mm(left, jnp.concatenate(split2(y), axis=0))
+    return r[:m] + r[m:]
+
+
+def nn3(x, y):
+    m = x.shape[0]
+    a, b, c = split3(x)
+    ya, yb, yc = split3(y)
+    r = mm(jnp.concatenate([a, b, c], axis=0), ya)
+    q = mm(jnp.concatenate([a, b], axis=0), yb)
+    return ((r[2 * m :] + mm(a, yc)) + q[m:]) + (r[m : 2 * m] + q[:m]) + r[:m]
+
+
+def nt2(x, y):
+    m, n = x.shape[0], y.shape[0]
+    r = lax.dot_general(
+        jnp.concatenate(split2(x), axis=0),
+        jnp.concatenate(split2(y), axis=0),
+        (((1,), (1,)), ((), ())),
+        preferred_element_type=F32,
+    )
+    r = r[:m] + r[m:]
+    return r[:, :n] + r[:, n:]
 
 
 def pivot_steps(d):
@@ -313,19 +347,25 @@
     )(block)
 
 
-def column_kernel(g_ref, inv_ref, diag_ref, z_ref, f_ref, c_ref):
+def column_kernel(g_ref, rows_ref, inv_ref, diag_ref, zc_ref, zp_ref, f_ref, c_ref):
     devices, extent, width = g_ref.shape
     share = width // devices
     for i in range(devices):
         for j in range((extent - share) // 8):
             c_ref[:, i * ((extent - share) // 8) + j, :] = g_ref[i, share + 8 * j : share + 8 * (j + 1), :]
-    z = nn(c_ref[4], inv_ref[...])
-    z_ref[...] = z
-    f_ref[...] = jnp.concatenate([nt(diag_ref[1 + t], z) for t in range(3)], axis=1)
-
-
-def panel_rows_of(ref, comp):
-    return jnp.concatenate([ref[piece, 0, comp] for piece in range(ref.shape[0])], axis=1)
+    tiles = rows_ref.shape[1]
+    v = jnp.concatenate([c_ref[4]] + [panel_rows_of(rows_ref, t, 0) for t in range(tiles)], axis=0)
+    z = nn3(v, inv_ref[...])
+    r = zc_ref.shape[0]
+    zc_ref[...] = z[:r]
+    for t in range(tiles):
+        zp_ref[t] = z[(1 + t) * r : (2 + t) * r]
+    f = nt(diag_ref[1:4].reshape(3 * share, width), z[:r])
+    f_ref[...] = jnp.concatenate([f[t * share : (t + 1) * share] for t in range(3)], axis=1)
+
+
+def panel_rows_of(ref, tile, comp):
+    return jnp.concatenate([ref[piece, tile, comp] for piece in range(ref.shape[0])], axis=1)
 
 
 def root_inverse(g):
@@ -363,66 +403,134 @@
 
 def prepare_kernel(
     prank_ref, crank_ref, trank_ref, krank_ref,
-    rows_ref, cols_ref, tr_ref, s_ref, inv_ref, zc_ref,
-    zp_ref, w_ref, h_ref, k_ref, ri_ref, q_ref,
+    rows_hbm, cols_hbm, tr_hbm, s_ref, zc_ref, zp_ref, f_hbm,
+    w_ref, h_ref, k_ref, ri_ref, q_ref,
+    rows_ref, cols_ref, tr_ref, f_ref, load_sem, send_sem, recv_sem, give_sem, take_sem,
 ):
-    tile = pl.program_id(0)
-    r = s_ref.shape[0]
+    row = lax.axis_index("row")
+    col = lax.axis_index("col")
+    devices = f_ref.shape[0]
+    core = lax.rem(row, 2)
+    pair = row + 1 - 2 * core
+    chips = devices // 2
+    tiles, r = zp_ref.shape[0], zp_ref.shape[1]
+    width = s_ref.shape[1]
+    others = [lax.rem(row + 2 * n, devices) for n in range(1, chips)]
+    sources = [lax.rem(row - 2 * n + devices, devices) for n in range(1, chips)]
+    barrier = pltpu.get_barrier_semaphore()
+    for to in others + [pair]:
+        pl.semaphore_signal(barrier, inc=1, device_id=(to, col), device_id_type=MESH)
+    loads = [
+        pltpu.make_async_copy(cols_hbm, cols_ref, load_sem.at[0]),
+        pltpu.make_async_copy(tr_hbm, tr_ref, load_sem.at[1]),
+        pltpu.make_async_copy(rows_hbm, rows_ref, load_sem.at[2]),
+        pltpu.make_async_copy(f_hbm, f_ref.at[row], load_sem.at[3]),
+    ]
+    for copy in loads:
+        copy.start()
+    pl.semaphore_wait(barrier, chips)
+
+    def remote(src, slot, to, ssem, rsem):
+        return pltpu.make_async_remote_copy(
+            src_ref=src, dst_ref=f_ref.at[slot], send_sem=ssem, recv_sem=rsem,
+            device_id=(to, col), device_id_type=MESH,
+        )
+
+    sends = [remote(f_hbm, row, to, send_sem.at[n], recv_sem.at[n]) for n, to in enumerate(others)]
+    for copy in sends:
+        copy.start()
+    gives = [remote(f_hbm, row, pair, give_sem.at[chips - 1], take_sem.at[chips - 1])]
+    gives[0].start()
+
+    loads[0].wait()
+    loads[1].wait()
+    s = s_ref[0:LIVE, :]
+    big = [cols_ref[t] for t in range(4)]
+    for i in range(tiles):
+        big += [tr_ref[i, 0, 4 + t] for t in range(4)]
+    hk = nt2(s, jnp.concatenate(big, axis=0))
+    live = lax.broadcasted_iota(jnp.int32, (LIVE, 4 * r), 0)
+    for i in range(tiles):
+        k = jnp.where(live < krank_ref[i, 0], hk[:, 0 : 4 * r], 0.0)
+        h = jnp.where(live < krank_ref[i, 0], hk[:, (1 + i) * 4 * r : (2 + i) * 4 * r], 0.0)
+        keep_t = lax.broadcasted_iota(jnp.int32, (LIVE, r), 1) < trank_ref[i, 0]
+        for t in range(4):
+            h_ref[i, t] = jnp.where(keep_t, h[:, t * r : (t + 1) * r], 0.0)
+            k_ref[i, t] = k[:, t * r : (t + 1) * r]
+    loads[2].wait()
     zc = zc_ref[...]
-    zp = nn(panel_rows_of(rows_ref, 4), inv_ref[...])
-    zp_ref[0] = zp
-    keep_p = lax.broadcasted_iota(jnp.int32, (r, r), 0) < prank_ref[tile]
-    keep_c = lax.broadcasted_iota(jnp.int32, (r, r), 1) < crank_ref[0]
-    keep = keep_p & keep_c
-    w0 = jnp.where(keep, nt(panel_rows_of(rows_ref, 4), zc), 0.0)
-    w_ref[0, 0] = w0
-    for t in range(3):
-        w_ref[0, 1 + t] = nt(panel_rows_of(rows_ref, 5 + t), zc) + nt(zp, cols_ref[5 + t])
-    live = (lax.broadcasted_iota(jnp.int32, (LIVE, s_ref.shape[1]), 0) < krank_ref[tile, 0]).astype(F32)
-    s = s_ref[0:LIVE, :] * live
-    keep_t = lax.broadcasted_iota(jnp.int32, (LIVE, r), 1) < trank_ref[tile, 0]
-    for t in range(4):
-        h_ref[0, t] = jnp.where(keep_t, nt(s, tr_ref[0, 0, 4 + t]), 0.0)
-        k_ref[0, t] = nt(s, cols_ref[t])
-    left = jnp.concatenate([h_ref[0, 0], -nt(k_ref[0, 0], w0)], axis=1)
-    up = jnp.concatenate([tr_ref[0, 0, 0], panel_rows_of(rows_ref, 0)], axis=0)
-    y = nn(left, up)
+    v = jnp.concatenate(
+        [panel_rows_of(rows_ref, i, 4 + t) for i in range(tiles) for t in range(4)], axis=0
+    )
+    w_all = nt2(v, zc)
     sub = lax.broadcasted_iota(jnp.int32, (LIVE, LIVE), 0)
     lane = lax.broadcasted_iota(jnp.int32, (LIVE, LIVE), 1)
-    g = nt(y, y) + ((sub == lane) & (sub >= krank_ref[tile, 0])).astype(F32)
-    ri = root_inverse(g)
-    ri_ref[0] = ri
-    q_ref[0] = nn(ri, y)
+    keeps = []
+    for i in range(tiles):
+        keeps.append(
+            (lax.broadcasted_iota(jnp.int32, (r, r), 0) < prank_ref[i])
+            & (lax.broadcasted_iota(jnp.int32, (r, r), 1) < crank_ref[0])
+        )
+        w0 = jnp.where(keeps[i], w_all[4 * i * r : (4 * i + 1) * r], 0.0)
+        w_ref[i, 0] = w0
+        left = jnp.concatenate([h_ref[i, 0], -nt(k_ref[i, 0], w0)], axis=1)
+        y = nn(left, jnp.concatenate([tr_ref[i, 0, 0], panel_rows_of(rows_ref, i, 0)], axis=0))
+        g = nt(y, y) + ((sub == lane) & (sub >= krank_ref[i, 0])).astype(F32)
+        ri = root_inverse(g)
+        ri_ref[i] = ri
+        q_ref[i] = nn(ri, y)
+    zp = jnp.concatenate([zp_ref[i] for i in range(tiles)], axis=0)
+    zv = nt2(zp, jnp.concatenate([cols_ref[5 + t] for t in range(3)], axis=0))
+
+    for n, source in enumerate(sources):
+        remote(f_hbm, source, pair, send_sem.at[n], recv_sem.at[n]).wait_recv()
+        gives.append(remote(f_ref.at[source], source, pair, give_sem.at[n], take_sem.at[n]))
+        gives[-1].start()
+    for n in range(1, chips):
+        slot = lax.rem(pair - 2 * n + devices, devices)
+        remote(f_hbm, slot, pair, give_sem.at[n - 1], take_sem.at[n - 1]).wait_recv()
+    remote(f_hbm, pair, pair, give_sem.at[chips - 1], take_sem.at[chips - 1]).wait_recv()
+    loads[3].wait()
+    zf = nn(zp, f_ref[...].reshape(width, f_ref.shape[2]))
+    for i in range(tiles):
+        for t in range(3):
+            dw = w_all[(4 * i + 1 + t) * r : (4 * i + 2 + t) * r]
+            part = zv[i * r : (i + 1) * r, t * r : (t + 1) * r] - zf[i * r : (i + 1) * r, t * r : (t + 1) * r]
+            w_ref[i, 1 + t] = jnp.where(keeps[i], dw + part, 0.0)
+    for copy in sends + gives:
+        copy.wait_send()
 
 
 def finish_kernel(
-    prank_ref, crank_ref, trank_ref,
-    rows_ref, cols_ref, tr_ref, f_ref, zp_ref, w_ref, h_ref, k_ref, ri_ref, q_ref,
-    o_ref,
+    trank_ref, rows_ref, cols_ref, tr_ref, w_ref, h_ref, k_ref, ri_ref, q_ref, o_ref
 ):
     tile = pl.program_id(0)
     r = h_ref.shape[3]
     width = q_ref.shape[2]
-    keep_p = lax.broadcasted_iota(jnp.int32, (r, r), 0) < prank_ref[tile]
-    keep_c = lax.broadcasted_iota(jnp.int32, (r, r), 1) < crank_ref[0]
-    keep = keep_p & keep_c
     keep_t = lax.broadcasted_iota(jnp.int32, (LIVE, r), 1) < trank_ref[tile, 0]
-    zf = nn(zp_ref[0], f_ref[...])
     w0 = w_ref[0, 0]
-    dw = [jnp.where(keep, w_ref[0, 1 + t] - zf[:, t * r : (t + 1) * r], 0.0) for t in range(3)]
+    dw = [w_ref[0, 1 + t] for t in range(3)]
     ri = ri_ref[0]
     q = q_ref[0]
     h = [h_ref[0, t] for t in range(4)]
-    k = [k_ref[0, t] for t in range(4)]
-    left0 = nn(ri, jnp.concatenate([h[0], -nt(k[0], w0)], axis=1))
-    left = [
-        nn(ri, jnp.concatenate([h[1 + t], -(nt(k[1 + t], w0) + nt(k[0], dw[t]))], axis=1))
-        for t in range(3)
+    k = jnp.concatenate([k_ref[0, t] for t in range(4)], axis=0)
+    kw = nt(k, w0)
+    kd = nt(k_ref[0, 0], jnp.concatenate(dw, axis=0))
+    left = [jnp.concatenate([h[0], -kw[0:LIVE]], axis=1)]
+    for t in range(3):
+        left.append(
+            jnp.concatenate(
+                [h[1 + t], -(kw[(1 + t) * LIVE : (2 + t) * LIVE] + kd[:, t * r : (t + 1) * r])], axis=1
+            )
+        )
+    left = nn(ri, jnp.concatenate(left, axis=1))
+    left0 = left[:, 0 : 2 * r]
+    ups = [
+        jnp.concatenate([tr_ref[0, 0, t], panel_rows_of(rows_ref, 0, t)], axis=0) for t in range(4)
     ]
-    ups = [jnp.concatenate([tr_ref[0, 0, t], panel_rows_of(rows_ref, t)], axis=0) for t in range(4)]
-    e = nn(jnp.concatenate(left, axis=0), ups[0])
-    e = e + jnp.concatenate([nn(left0, ups[1 + t]) for t in range(3)], axis=0)
-    m = nt(e, q)
+    e = nn2(jnp.concatenate([left[:, 2 * r * t : 2 * r * (t + 1)] for t in (1, 2, 3)], axis=0), ups[0])
+    e = e + jnp.concatenate([nn2(left0, ups[1 + t]) for t in range(3)], axis=0)
+    m = nt2(e, q)
     sub = lax.broadcasted_iota(jnp.int32, (LIVE, LIVE), 0)
     lane = lax.broadcasted_iota(jnp.int32, (LIVE, LIVE), 1)
     phi = []
@@ -432,21 +540,21 @@
         phi.append(jnp.where(sub > lane, mid, jnp.where(sub == lane, 0.5 * mid, 0.0)))
     dq = e - nn(jnp.concatenate(phi, axis=0), q)
     qs = jnp.concatenate([q, dq], axis=0)
-    js = nt(qs, ups[0])
-    extra = [nt(q, ups[1 + t]) for t in range(3)]
-    j0 = js[0:LIVE]
-    j0u, j0p = jnp.where(keep_t, j0[:, :r], 0.0), j0[:, r:]
-    n0 = jnp.concatenate([j0u, -nn(j0p, w0)], axis=1)
-    ns = [n0]
-    for t in range(3):
-        jt = js[(1 + t) * LIVE : (2 + t) * LIVE] + extra[t]
-        ns.append(
-            jnp.concatenate(
-                [jnp.where(keep_t, jt[:, :r], 0.0), -(nn(jt[:, r:], w0) + nn(j0p, dw[t]))], axis=1
-            )
-        )
+    js = nt2(qs, ups[0])
+    extra = nt2(q, jnp.concatenate(ups[1:], axis=0))
+    js = [js[0:LIVE]] + [
+        js[(1 + t) * LIVE : (2 + t) * LIVE] + extra[:, 2 * r * t : 2 * r * (t + 1)] for t in range(3)
+    ]
+    jw = nn(jnp.concatenate([j[:, r:] for j in js], axis=0), w0)
+    jd = nn(js[0][:, r:], jnp.concatenate(dw, axis=1))
+    ns = []
+    for t in range(4):
+        b = jw[t * LIVE : (t + 1) * LIVE]
+        if t:
+            b = b + jd[:, (t - 1) * r : t * r]
+        ns.append(jnp.concatenate([jnp.where(keep_t, js[t][:, :r], 0.0), -b], axis=1))
     vs = [jnp.concatenate([tr_ref[0, 0, 4 + t], cols_ref[t]], axis=0) for t in range(4)]
-    b = nn(jnp.concatenate(ns, axis=0), vs[0])
+    b = nn2(jnp.concatenate(ns, axis=0), vs[0])
     up_scale = math.sqrt(width)
     down_scale = 1.0 / math.sqrt(r)
     zero = jnp.zeros((r - LIVE, width), F32)
@@ -454,7 +562,7 @@
         o_ref[0, 0, t, 0:LIVE, :] = qs[t * LIVE : (t + 1) * LIVE] * up_scale
         bt = b[t * LIVE : (t + 1) * LIVE]
         if t:
-            bt = bt + nn(n0, vs[t])
+            bt = bt + nn2(ns[0], vs[t])
         o_ref[0, 0, 4 + t, 0:LIVE, :] = bt * down_scale
         o_ref[0, 0, t, LIVE:r, :] = zero
         o_ref[0, 0, 4 + t, LIVE:r, :] = zero
@@ -497,53 +605,75 @@
         cost_estimate=cost(60e9, 8 << 20),
         name="invert",
     )(gathered)
-    zc, f, cols = pl.pallas_call(
+    vmem = pl.BlockSpec(memory_space=pltpu.VMEM)
+    hbm = pl.BlockSpec(memory_space=pl.ANY)
+    smem = pl.BlockSpec(memory_space=pltpu.SMEM)
+    v_spec = pl.BlockSpec(
+        (pieces, tiles, 1) + rows.shape[3:], lambda i: (0, 0, 4, 0, 0)
+    )
+    outs = dict(
+        zc=(rank, width),
+        zp=(tiles, rank, width),
+        f=(diag.shape[1], 3 * rank),
+        cols=(panel_cols.shape[1], rank, width),
+    )
+    zc, zp, f, cols = pl.pallas_call(
         column_kernel,
-        out_shape=(
-            jax.ShapeDtypeStruct((rank, width), F32),
-            jax.ShapeDtypeStruct((diag.shape[1], 3 * rank), F32),
-            jax.ShapeDtypeStruct((panel_cols.shape[1], rank, width), F32),
-        ),
+        grid=(1,),
+        in_specs=[whole(gathered.shape), v_spec, whole(inverse.shape), whole(diag.shape)],
+        out_specs=[whole(v) for v in outs.values()],
+        out_shape=[jax.ShapeDtypeStruct(v, F32) for v in outs.values()],
         compiler_params=params(),
         cost_estimate=cost(2e9, 6 << 20),
         name="columns",
-    )(gathered, inverse, diag)
-    f_all = gather(f, 2).reshape(width, 3 * rank)
-    smem = pl.BlockSpec(memory_space=pltpu.SMEM)
-    rows_spec = pl.BlockSpec((pieces, 1) + rows.shape[2:], lambda i: (0, i, 0, 0, 0))
-    tr_spec = tiled((1,) + trailing.shape[1:])
+    )(gathered, rows, inverse, diag)
     mids = dict(
-        zp=(tiles, rank, width),
         w=(tiles, 4, rank, rank),
         h=(tiles, 4, LIVE, rank),
         k=(tiles, 4, LIVE, rank),
         ri=(tiles, LIVE, LIVE),
         q=(tiles, LIVE, width),
     )
-    mid_specs = [tiled((1,) + s[1:]) for s in mids.values()]
+    devices = lax.axis_size("row")
     mid = pl.pallas_call(
         prepare_kernel,
-        grid=(tiles,),
-        in_specs=[smem] * 4
-        + [rows_spec, whole(cols.shape), tr_spec, whole(sketch.shape), whole(inverse.shape), whole(zc.shape)],
-        out_specs=mid_specs,
-        out_shape=[jax.ShapeDtypeStruct(s, F32) for s in mids.values()],
-        compiler_params=params(),
+        in_specs=[smem] * 4 + [hbm] * 3 + [vmem] * 3 + [hbm],
+        out_specs=[vmem] * len(mids),
+        out_shape=[jax.ShapeDtypeStruct(v, F32) for v in mids.values()],
+        scratch_shapes=[
+            pltpu.VMEM(rows.shape, F32),
+            pltpu.VMEM(cols.shape, F32),
+            pltpu.VMEM(trailing.shape, F32),
+            pltpu.VMEM((devices,) + f.shape, F32),
+            pltpu.SemaphoreType.DMA((4,)),
+            pltpu.SemaphoreType.DMA((devices // 2 - 1,)),
+            pltpu.SemaphoreType.DMA((devices // 2 - 1,)),
+            pltpu.SemaphoreType.DMA((devices // 2,)),
+            pltpu.SemaphoreType.DMA((devices // 2,)),
+        ],
+        compiler_params=pltpu.CompilerParams(
+            vmem_limit_bytes=56 << 20, collective_id=2, has_side_effects=True
+        ),
         cost_estimate=cost(10e9, 20 << 20),
         name="prepare",
-    )(panel_rank, col_rank, tile_rank, keep_rank, rows, cols, trailing, sketch, inverse, zc)
+    )(panel_rank, col_rank, tile_rank, keep_rank, rows, cols, trailing, sketch, zc, zp, f)
+    tr_spec = tiled((1,) + trailing.shape[1:])
     return pl.pallas_call(
         finish_kernel,
         grid=(tiles,),
-        in_specs=[smem] * 3
-        + [rows_spec, whole(cols.shape), tr_spec, whole(f_all.shape)]
-        + mid_specs,
+        in_specs=[
+            smem,
+            pl.BlockSpec((pieces, 1, 4) + rows.shape[3:], lambda i: (0, i, 0, 0, 0)),
+            pl.BlockSpec((4,) + cols.shape[1:], lambda i: (0, 0, 0)),
+            tr_spec,
+        ]
+        + [tiled((1,) + v[1:]) for v in mids.values()],
         out_specs=tr_spec,
         out_shape=jax.ShapeDtypeStruct(trailing.shape, F32),
         compiler_params=params(),
         cost_estimate=cost(10e9, 20 << 20),
         name="finish",
-    )(panel_rank, col_rank, tile_rank, rows, cols, trailing, f_all, *mid)
+    )(tile_rank, rows, cols, trailing, *mid)
 
 
 def solution(mesh):

time: 183 us -> 148 us (0.81)
  Pallas kernels: 164 us -> 129 us
    pallas_call x2 -> x1, Pallas kernels: 46.4 us -> 28.6 us  [gather(): pl.pallas_call(gather_kernel, out_shape=jax.ShapeDtypeStruct((devices,) +...]
    pallas_call x3, Pallas kernels: 54.5 us -> 37.3 us  [the longest x1 17.6 us: on_device(): pl.pallas_call(prepare_kernel, in_specs=[smem] * 4 + [hbm] * 3 + [vmem] *...]
  transfers between devices with their start and end apart: 1 -> 1, of which waited for: 0 -> 0; matrix products, arithmetic and copies ran while one was open for 2% -> 3% of each run, Pallas kernels for 65% -> 62%
where the time goes in v3:
time: 148 us
  Pallas kernels  129 us (87%)
  between operations  14.1 us (10%)
  local copies, waits for them, and re-layouts  3.04 us (2%)
    pallas_call x1, Pallas kernels, on_device(): pl.pallas_call(invert_kernel, out_shape=jax.ShapeDtypeStruct((width, widt...  63.1 us
    pallas_call x1, Pallas kernels, gather(): pl.pallas_call(gather_kernel, out_shape=jax.ShapeDtypeStruct((devices,) +...  28.6 us
    pallas_call x1, Pallas kernels, on_device(): pl.pallas_call(prepare_kernel, in_specs=[smem] * 4 + [hbm] * 3 + [vmem] *...  17.6 us
    pallas_call x1, Pallas kernels, on_device(): pl.pallas_call(finish_kernel, grid=(tiles,), in_specs=[smem, pl.BlockSpec...  11 us
    pallas_call x1, Pallas kernels, on_device(): pl.pallas_call(column_kernel, grid=(1,), in_specs=[whole(gathered.shape),...  8.69 us
  transfers between devices with their start and end apart: 1, of which 0 were waited for; matrix products, arithmetic and copies ran while one was open for 3% of the time, Pallas kernels for 62%

profile of v3, /device:TPU:1, one launch (start us, length us, event | category | flops | bytes accessed | tf_op | source)
XLA Modules:
  0.0 147.5 jit_solution(3465313668893004542)
XLA Ops:
  6.5 0.0 copy-start
  6.5 0.0 copy-start.1
  6.5 0.0 all-gather.3.cloned.1.call-start
  6.5 0.7 all-gather.3.cloned.1.call-update
  7.3 0.9 copy.19
  8.1 0.9 slice_bitcast_fusion
  9.0 0.7 pad_maximum_fusion.x_ref
  9.7 28.6 %gather.1.g_ref = f32[32,48,1024]{2,1,0:T(8,128)} custom-call(f32[48,1024]{1,0:T(8,128)} %pad_maximum_fusion.x_ref), custom_call_target="tpu_custom_call" | custom-call | bytes 12582912 | tf_op jit(solution)/shard_map/gather/pallas_call | solution.py:332
  38.4 0.0 copy-done
  38.4 0.6 copy.17.trank_ref
  39.0 0.0 copy-done.1
  39.0 0.6 copy.16.krank_ref
  40.3 63.1 %invert.1.inv_ref = f32[1024,1024]{1,0:T(8,128)} custom-call(f32[32,48,1024]{2,1,0:T(8,128)} %gather.1.g_ref), custom_call_target="tpu_custom_call" | custom-call | flops 60000002048 | bytes 8388608 | tf_op jit(solution)/shard_map/invert/pallas_call | solution.py:596
  103.4 0.0 all-gather.3.cloned.1.call-done
  103.4 8.7 %columns.1 = (f32[64,1024]{1,0:T(8,128)}, f32[2,64,1024]{2,1,0:T(8,128)}, f32[32,192]{1,0:T(8,128)}, f32[8,64,1024]{2,1,0:T(8,128)}) custom-call(f32[32,48,1024]{2,1,0:T(8,128)} %gather.1.g_ref, f32[8,2,8,64,128]{4,3,2,1,0:T(8,128)} %bitcast.9, f32[1024,1024]{1,0:T(8,128)} %invert.1.inv_ref, f32[4,32,1024]{2,1,0:T(8,128)} %diag_ref.1), custom_call_target="tpu_custom_call" | custom-call | flops 2000000000 | bytes 6291456 | tf_op jit(solution)/shard_map/columns/pallas_call | solution.py:620
  112.1 17.6 %prepare.1 = (f32[2,4,64,64]{3,2,1,0:T(8,128)}, f32[2,4,32,64]{3,2,1,0:T(8,128)}, f32[2,4,32,64]{3,2,1,0:T(8,128)}, f32[2,32,32]{2,1,0:T(8,128)}, f32[2,32,1024]{2,1,0:T(8,128)}) custom-call(s32[2]{0:T(128)} %prank_ref.1, s32[1]{0:T(128)S(6)} %copy.20.crank_ref, s32[2,1]{1,0:T(2,128)} %copy.17.trank_ref, s32[2,1]{1,0:T(2,128)} %copy.16.krank_ref, ...), custom_call_target="tpu_custom_call" | custom-call | flops 10000000000 | bytes 20971520 | tf_op jit(solution)/shard_map/prepare/pallas_call | solution.py:638
  129.7 11.0 %finish.1 = f32[2,1,8,64,1024]{4,3,2,1,0:T(8,128)} custom-call(s32[2,1]{1,0:T(2,128)} %copy.17.trank_ref, f32[8,2,8,64,128]{4,3,2,1,0:T(8,128)} %bitcast.11, f32[8,64,1024]{2,1,0:T(8,128)} %get-tuple-element.14.cols_hbm.cols_ref, f32[2,1,8,64,1024]{4,3,2,1,0:T(8,128)} %tr_ref.1, f32[2,4,64,64]{3,2,1,0:T(8,128)} %get-tuple-element.18.w_ref, ...), custom_call_target="tpu_custom_call" | custom-call | flops 10000000000 | bytes 20971520 | tf_op jit(solution)/shard_map/finish/pallas_call | solution.py:661
Async XLA Ops:
  6.5 31.8 %copy-start = (s32[2,1]{0,1:T(1,128)S(1)}, s32[2,1]{0,1:T(1,128)}, u32[]{:S(2)}) copy-start(s32[2,1]{0,1:T(1,128)} %param.16) | copy-start | bytes 28
  6.5 32.5 %copy-start.1 = (s32[2,1]{0,1:T(1,128)S(1)}, s32[2,1]{0,1:T(1,128)}, u32[]{:S(2)}) copy-start(s32[2,1]{0,1:T(1,128)} %param.17) | copy-start | bytes 28
  6.5 96.9 %all-gather.3.cloned.1.call-start = ((), (), s32[]{:S(2)}) async-start(), calls=%async_computation | async-start | bytes 4718592 | tf_op jit(solution)/shard_map/all_gather | solution.py:593
Sparse Core Ops, SparseCore 0:
  9.1 58.3 all-gather.2

commit v4 on v3

--- a/solution.py
+++ b/solution.py
@@ -123,32 +123,51 @@
 
 
 def pivot_steps(d):
-    n = d.shape[0]
-    lane = lax.broadcasted_iota(jnp.int32, (n, n), 1)
-    sub = lax.broadcasted_iota(jnp.int32, (n, n), 0)
+    n, half = d.shape[0], NPIV // 2
+    sub8 = lax.broadcasted_iota(jnp.int32, (8, n), 0)
     lane8 = lax.broadcasted_iota(jnp.int32, (8, n), 1)
-    for j in range(0, n, NPIV):
+    v = [d[8 * i : 8 * i + 8, :] for i in range(n // 8)]
+    for g in range(n // 8):
+        j = NPIV * g
+        cols = [jnp.broadcast_to(v[g][:, j + q : j + q + 1], (8, n)) for q in range(NPIV)]
         m = [[None] * NPIV for _ in range(NPIV)]
         for r in range(NPIV):
             for c in range(r, NPIV):
-                m[r][c] = jnp.broadcast_to(d[j + r : j + r + 1, j + c : j + c + 1], (8, n))
+                m[r][c] = jnp.broadcast_to(cols[c][r : r + 1, :], (8, n))
                 m[c][r] = m[r][c]
-        cols = [jnp.broadcast_to(d[:, j + q : j + q + 1], (n, n)) for q in range(NPIV)]
-        p = small_inverse(m)
         own = (lane8 >= j) & (lane8 < j + NPIV)
         rows = [
-            jnp.where(own, (lane8 == j + q).astype(F32), jnp.broadcast_to(d[j + q : j + q + 1, :], (8, n)))
+            jnp.where(own, (lane8 == j + q).astype(F32), jnp.broadcast_to(v[g][q : q + 1, :], (8, n)))
             for q in range(NPIV)
         ]
-        new = [total(p[q][k] * rows[k] for k in range(NPIV)) for q in range(NPIV)]
-        new = [jnp.concatenate([t] * (n // 8), axis=0) for t in new]
-        out = jnp.where((lane >= j) & (lane < j + NPIV), 0.0, d)
-        for q in range(NPIV):
-            out = out - cols[q] * new[q]
-        for q in range(NPIV):
-            out = jnp.where(sub == j + q, new[q], out)
-        d = out
-        yield d
+        span = range(half)
+        e = small_inverse([row[:half] for row in m[:half]])
+        b = [row[half:] for row in m[:half]]
+        x = [[total(e[i][k] * b[k][q] for k in span) for q in span] for i in span]
+        s = [[None] * half for _ in span]
+        for i in span:
+            for q in range(i, half):
+                s[i][q] = m[half + i][half + q] - total(b[k][i] * x[k][q] for k in span)
+                s[q][i] = s[i][q]
+        f = small_inverse(s)
+        top = [total(e[i][k] * rows[k] for k in span) for i in span]
+        low = [rows[half + i] - total(b[k][i] * top[k] for k in span) for i in span]
+        low = [total(f[i][k] * low[k] for k in span) for i in span]
+        new = [top[i] - total(x[i][k] * low[k] for k in span) for i in span] + low
+        out = [None] * len(v)
+        first = (g + 1) % len(v)
+        for i in [first] + [k for k in range(len(v)) if k != first]:
+            if i == g:
+                t = new[0]
+                for q in range(1, NPIV):
+                    t = jnp.where(sub8 == q, new[q], t)
+            else:
+                t = jnp.where(own, 0.0, v[i])
+                for q in list(range(half, NPIV)) + list(range(half)):
+                    t = t - jnp.broadcast_to(v[i][:, j + q : j + q + 1], (8, n)) * new[q]
+            out[i] = t
+        v = out
+        yield jnp.concatenate(v, axis=0)
 
 
 def invert_kernel(g_ref, o_ref, p_ref, l_ref, r_ref):
@@ -451,9 +470,9 @@
     hk = nt2(s, jnp.concatenate(big, axis=0))
     live = lax.broadcasted_iota(jnp.int32, (LIVE, 4 * r), 0)
     for i in range(tiles):
-        k = jnp.where(live < krank_ref[i, 0], hk[:, 0 : 4 * r], 0.0)
-        h = jnp.where(live < krank_ref[i, 0], hk[:, (1 + i) * 4 * r : (2 + i) * 4 * r], 0.0)
-        keep_t = lax.broadcasted_iota(jnp.int32, (LIVE, r), 1) < trank_ref[i, 0]
+        k = jnp.where(live < krank_ref[i], hk[:, 0 : 4 * r], 0.0)
+        h = jnp.where(live < krank_ref[i], hk[:, (1 + i) * 4 * r : (2 + i) * 4 * r], 0.0)
+        keep_t = lax.broadcasted_iota(jnp.int32, (LIVE, r), 1) < trank_ref[i]
         for t in range(4):
             h_ref[i, t] = jnp.where(keep_t, h[:, t * r : (t + 1) * r], 0.0)
             k_ref[i, t] = k[:, t * r : (t + 1) * r]
@@ -475,7 +494,7 @@
         w_ref[i, 0] = w0
         left = jnp.concatenate([h_ref[i, 0], -nt(k_ref[i, 0], w0)], axis=1)
         y = nn(left, jnp.concatenate([tr_ref[i, 0, 0], panel_rows_of(rows_ref, i, 0)], axis=0))
-        g = nt(y, y) + ((sub == lane) & (sub >= krank_ref[i, 0])).astype(F32)
+        g = nt(y, y) + ((sub == lane) & (sub >= krank_ref[i])).astype(F32)
         ri = root_inverse(g)
         ri_ref[i] = ri
         q_ref[i] = nn(ri, y)
@@ -507,7 +526,7 @@
     tile = pl.program_id(0)
     r = h_ref.shape[3]
     width = q_ref.shape[2]
-    keep_t = lax.broadcasted_iota(jnp.int32, (LIVE, r), 1) < trank_ref[tile, 0]
+    keep_t = lax.broadcasted_iota(jnp.int32, (LIVE, r), 1) < trank_ref[tile]
     w0 = w_ref[0, 0]
     dw = [w_ref[0, 1 + t] for t in range(3)]
     ri = ri_ref[0]
@@ -589,6 +608,7 @@
 ):
     rank, width = sketch.shape
     tiles = trailing.shape[0]
+    tile_rank, keep_rank = tile_rank.reshape(-1), keep_rank.reshape(-1)
     pieces = lax.axis_size("col")
     rows = lax.all_gather(panel_rows, "col", axis=0, tiled=False)
     own_cols = panel_cols[0].transpose(1, 0, 2).reshape(-1, width)

time: 148 us -> 137 us (0.926)
  Pallas kernels: 129 us -> 120 us
    pallas_call x1, Pallas kernels: 63.1 us -> 53.8 us  [on_device(): pl.pallas_call(invert_kernel, out_shape=jax.ShapeDtypeStruct((width, widt...]
  transfers between devices with their start and end apart: 1 -> 1, of which waited for: 0 -> 0; matrix products, arithmetic and copies ran while one was open for 3% -> 2% of each run, Pallas kernels for 62% -> 60%
where the time goes in v4:
time: 137 us
  Pallas kernels  120 us (88%)
  between operations  14.1 us (10%)
  local copies, waits for them, and re-layouts  1.78 us (1%)
    pallas_call x1, Pallas kernels, on_device(): pl.pallas_call(invert_kernel, out_shape=jax.ShapeDtypeStruct((width, widt...  53.8 us
    pallas_call x1, Pallas kernels, gather(): pl.pallas_call(gather_kernel, out_shape=jax.ShapeDtypeStruct((devices,) +...  28.6 us
    pallas_call x1, Pallas kernels, on_device(): pl.pallas_call(prepare_kernel, in_specs=[smem] * 4 + [hbm] * 3 + [vmem] *...  17.6 us
    pallas_call x1, Pallas kernels, on_device(): pl.pallas_call(finish_kernel, grid=(tiles,), in_specs=[smem, pl.BlockSpec...  11 us
    pallas_call x1, Pallas kernels, on_device(): pl.pallas_call(column_kernel, grid=(1,), in_specs=[whole(gathered.shape),...  8.69 us
  transfers between devices with their start and end apart: 1, of which 0 were waited for; matrix products, arithmetic and copies ran while one was open for 2% of the time, Pallas kernels for 60%

profile of v4, /device:TPU:1, one launch (start us, length us, event | category | flops | bytes accessed | tf_op | source)
XLA Modules:
  0.0 137.0 jit_solution(12813102215145097124)
XLA Ops:
  6.5 0.0 all-gather.3.cloned.1.call-start
  6.5 0.7 all-gather.3.cloned.1.call-update
  7.3 0.9 copy.13
  8.1 0.9 slice_bitcast_fusion
  9.0 0.7 pad_maximum_fusion.x_ref
  9.7 28.6 %gather.1.g_ref = f32[32,48,1024]{2,1,0:T(8,128)} custom-call(f32[48,1024]{1,0:T(8,128)} %pad_maximum_fusion.x_ref), custom_call_target="tpu_custom_call" | custom-call | bytes 12582912 | tf_op jit(solution)/shard_map/gather/pallas_call | solution.py:351
  39.0 53.8 %invert.1.inv_ref = f32[1024,1024]{1,0:T(8,128)} custom-call(f32[32,48,1024]{2,1,0:T(8,128)} %gather.1.g_ref), custom_call_target="tpu_custom_call" | custom-call | flops 60000002048 | bytes 8388608 | tf_op jit(solution)/shard_map/invert/pallas_call | solution.py:616
  92.8 0.0 all-gather.3.cloned.1.call-done
  92.8 8.7 %columns.1 = (f32[64,1024]{1,0:T(8,128)}, f32[2,64,1024]{2,1,0:T(8,128)}, f32[32,192]{1,0:T(8,128)}, f32[8,64,1024]{2,1,0:T(8,128)}) custom-call(f32[32,48,1024]{2,1,0:T(8,128)} %gather.1.g_ref, f32[8,2,8,64,128]{4,3,2,1,0:T(8,128)} %bitcast.11, f32[1024,1024]{1,0:T(8,128)} %invert.1.inv_ref, f32[4,32,1024]{2,1,0:T(8,128)} %diag_ref.1), custom_call_target="tpu_custom_call" | custom-call | flops 2000000000 | bytes 6291456 | tf_op jit(solution)/shard_map/columns/pallas_call | solution.py:640
  101.5 17.6 %prepare.1 = (f32[2,4,64,64]{3,2,1,0:T(8,128)}, f32[2,4,32,64]{3,2,1,0:T(8,128)}, f32[2,4,32,64]{3,2,1,0:T(8,128)}, f32[2,32,32]{2,1,0:T(8,128)}, f32[2,32,1024]{2,1,0:T(8,128)}) custom-call(s32[2]{0:T(128)} %prank_ref.1, s32[1]{0:T(128)S(6)} %copy.14.crank_ref, s32[2]{0:T(128)} %bitcast.17, s32[2]{0:T(128)} %bitcast.16, f32[8,2,8,64,128]{4,3,2,1,0:T(8,128)} %bitcast.12, ...), custom_call_target="tpu_custom_call" | custom-call | flops 10000000000 | bytes 20971520 | tf_op jit(solution)/shard_map/prepare/pallas_call | solution.py:658
  119.1 11.0 %finish.1 = f32[2,1,8,64,1024]{4,3,2,1,0:T(8,128)} custom-call(s32[2]{0:T(128)} %bitcast.18, f32[8,2,8,64,128]{4,3,2,1,0:T(8,128)} %bitcast.13, f32[8,64,1024]{2,1,0:T(8,128)} %get-tuple-element.14.cols_hbm.cols_ref, f32[2,1,8,64,1024]{4,3,2,1,0:T(8,128)} %tr_ref.1, f32[2,4,64,64]{3,2,1,0:T(8,128)} %get-tuple-element.18.w_ref, ...), custom_call_target="tpu_custom_call" | custom-call | flops 10000000000 | bytes 20971520 | tf_op jit(solution)/shard_map/finish/pallas_call | solution.py:681
Async XLA Ops:
  6.5 86.3 %all-gather.3.cloned.1.call-start = ((), (), s32[]{:S(2)}) async-start(), calls=%async_computation | async-start | bytes 4718592 | tf_op jit(solution)/shard_map/all_gather | solution.py:613
Sparse Core Ops, SparseCore 0:
  9.1 58.3 all-gather.2

commit v5 on v4

--- a/solution.py
+++ b/solution.py
@@ -170,12 +170,9 @@
         yield jnp.concatenate(v, axis=0)
 
 
-def invert_kernel(g_ref, o_ref, p_ref, l_ref, r_ref):
+def invert(o_ref, p_ref, l_ref, r_ref, between):
     size = o_ref.shape[0]
     blocks = size // BLOCK
-    share = size // g_ref.shape[0]
-    for i in range(g_ref.shape[0]):
-        o_ref[i * share : (i + 1) * share, :] = g_ref[i, 0:share, :]
     d = None
     for d in pivot_steps(o_ref[0:BLOCK, 0:BLOCK]):
         pass
@@ -221,6 +218,7 @@
             p_ref[...] = found
 
     def body(k, carry):
+        between(k)
         step(k, False)
         return carry
 
@@ -228,7 +226,11 @@
     step(blocks - 1, True)
 
 
-def gather_kernel(x_ref, o_ref, stage_ref, local_sem, send_sem, recv_sem, pair_sem):
+def factor_kernel(
+    x_ref, panel_ref, o_ref, rows_ref, inv_ref,
+    stage_ref, stage2_ref, p_ref, l_ref, r_ref,
+    local_sem, send_sem, recv_sem, pair_sem, load_sem, zsend_sem, zrecv_sem,
+):
     row = lax.axis_index("row")
     col = lax.axis_index("col")
     core = lax.rem(row, 2)
@@ -250,13 +252,51 @@
         "pair": device(0, 0, 1 - core),
     }
     shift = {"a+": (1, 0), "a-": (-1, 0), "b+": (0, 1), "b-": (0, -1)}
+    depth = rows_ref.shape[0]
+    ahead, back = lax.rem(col + 1, depth), lax.rem(col + depth - 1, depth)
     barrier = pltpu.get_barrier_semaphore()
     for to in peers.values():
         pl.semaphore_signal(barrier, inc=1, device_id=(to, col), device_id_type=MESH)
-    pl.semaphore_wait(barrier, len(peers))
+    for to in (ahead, back):
+        pl.semaphore_signal(barrier, inc=1, device_id=(row, to), device_id_type=MESH)
+    pl.semaphore_wait(barrier, len(peers) + 2)
 
     mine = pltpu.make_async_copy(x_ref, stage_ref, local_sem.at[0])
     mine.start()
+    mine2 = pltpu.make_async_copy(panel_ref, stage2_ref, local_sem.at[2])
+    mine2.start()
+
+    def ring(dist, up, h=None):
+        owner = lax.rem(col - dist + depth, depth) if up else lax.rem(col + dist, depth)
+        source = panel_ref if dist == 0 else rows_ref.at[owner]
+        target = rows_ref.at[owner]
+        if h is not None:
+            source, target = source.at[h], target.at[h]
+        return pltpu.make_async_remote_copy(
+            src_ref=source,
+            dst_ref=target,
+            send_sem=zsend_sem.at[dist, 0 if up else 1],
+            recv_sem=zrecv_sem.at[dist, 0 if up else 1],
+            device_id=(row, ahead if up else back),
+            device_id_type=MESH,
+        )
+
+    def landed(dist, up, h=None):
+        owner = lax.rem(col - dist - 1 + depth, depth) if up else lax.rem(col + dist + 1, depth)
+        target = rows_ref.at[owner]
+        if h is not None:
+            target = target.at[h]
+        pltpu.make_async_remote_copy(
+            src_ref=target,
+            dst_ref=target,
+            send_sem=zsend_sem.at[dist, 0 if up else 1],
+            recv_sem=zrecv_sem.at[dist, 0 if up else 1],
+            device_id=(row, ahead if up else back),
+            device_id_type=MESH,
+        ).wait_recv()
+
+    ring(0, True).start()
+    ring(0, False).start()
     sent = []
 
     def part(ref, h):
@@ -332,6 +372,48 @@
     for copy in sent:
         copy.wait_send()
     keep.wait()
+    mine2.wait()
+    keep2 = pltpu.make_async_copy(stage2_ref, rows_ref.at[col], local_sem.at[3])
+    keep2.start()
+    landed(0, True)
+    landed(0, False)
+    ring(1, True).start()
+    ring(1, False).start()
+    devices = o_ref.shape[0]
+    share = inv_ref.shape[0] // devices
+    loads = [
+        pltpu.make_async_copy(
+            o_ref.at[i, pl.ds(0, share)], inv_ref.at[pl.ds(i * share, share)], load_sem.at[i]
+        )
+        for i in range(devices)
+    ]
+    for copy in loads:
+        copy.start()
+    for copy in loads:
+        copy.wait()
+
+    def between(k):
+        @pl.when(k == 2)
+        def _():
+            landed(1, True)
+            landed(1, False)
+            ring(2, True).start()
+            ring(2, False).start()
+
+        @pl.when(k == 4)
+        def _():
+            landed(2, True)
+            landed(2, False)
+            ring(3, True, 0).start()
+            ring(3, False, 1).start()
+
+    invert(inv_ref, p_ref, l_ref, r_ref, between)
+    landed(3, True, 0)
+    landed(3, False, 1)
+    for dist in range(4):
+        ring(dist, True, 0 if dist == 3 else None).wait_send()
+        ring(dist, False, 1 if dist == 3 else None).wait_send()
+    keep2.wait()
 
 
 def arrive_pair(o_ref, device, pair_sem, send_sem, i1, i2, core, pair, col):
@@ -344,26 +426,6 @@
         device_id=(pair, col),
         device_id_type=MESH,
     ).wait_recv()
-
-
-def gather(block, collective_id):
-    devices = lax.axis_size("row")
-    return pl.pallas_call(
-        gather_kernel,
-        out_shape=jax.ShapeDtypeStruct((devices,) + block.shape, F32),
-        in_specs=[pl.BlockSpec(memory_space=pl.ANY)],
-        out_specs=pl.BlockSpec(memory_space=pl.ANY),
-        scratch_shapes=[
-            pltpu.VMEM(block.shape, F32),
-            pltpu.SemaphoreType.DMA((2,)),
-            pltpu.SemaphoreType.DMA((SENDS,)),
-            pltpu.SemaphoreType.DMA((SIDE, SIDE, 2)),
-            pltpu.SemaphoreType.DMA((SIDE, SIDE)),
-        ],
-        compiler_params=pltpu.CompilerParams(collective_id=collective_id, has_side_effects=True),
-        cost_estimate=cost(0, 12 << 20),
-        name="gather",
-    )(block)
 
 
 def column_kernel(g_ref, rows_ref, inv_ref, diag_ref, zc_ref, zp_ref, f_ref, c_ref):
@@ -610,21 +672,38 @@
     tiles = trailing.shape[0]
     tile_rank, keep_rank = tile_rank.reshape(-1), keep_rank.reshape(-1)
     pieces = lax.axis_size("col")
-    rows = lax.all_gather(panel_rows, "col", axis=0, tiled=False)
     own_cols = panel_cols[0].transpose(1, 0, 2).reshape(-1, width)
-    gathered = gather(jnp.concatenate([diag[0], own_cols], axis=0), 1)
-    inverse = pl.pallas_call(
-        invert_kernel,
-        out_shape=jax.ShapeDtypeStruct((width, width), F32),
+    block = jnp.concatenate([diag[0], own_cols], axis=0)
+    devices = lax.axis_size("row")
+    gathered, rows, inverse = pl.pallas_call(
+        factor_kernel,
+        in_specs=[pl.BlockSpec(memory_space=pl.ANY)] * 2,
+        out_specs=[pl.BlockSpec(memory_space=pl.ANY)] * 2 + [pl.BlockSpec(memory_space=pltpu.VMEM)],
+        out_shape=[
+            jax.ShapeDtypeStruct((devices,) + block.shape, F32),
+            jax.ShapeDtypeStruct((pieces,) + panel_rows.shape, F32),
+            jax.ShapeDtypeStruct((width, width), F32),
+        ],
         scratch_shapes=[
+            pltpu.VMEM(block.shape, F32),
+            pltpu.VMEM(panel_rows.shape, F32),
             pltpu.VMEM((BLOCK, BLOCK), F32),
             pltpu.VMEM((width, 3 * BLOCK), BF16),
             pltpu.VMEM((3 * BLOCK, width), BF16),
+            pltpu.SemaphoreType.DMA((4,)),
+            pltpu.SemaphoreType.DMA((SENDS,)),
+            pltpu.SemaphoreType.DMA((SIDE, SIDE, 2)),
+            pltpu.SemaphoreType.DMA((SIDE, SIDE)),
+            pltpu.SemaphoreType.DMA((devices,)),
+            pltpu.SemaphoreType.DMA((4, 2)),
+            pltpu.SemaphoreType.DMA((4, 2)),
         ],
-        compiler_params=params(),
-        cost_estimate=cost(60e9, 8 << 20),
-        name="invert",
-    )(gathered)
+        compiler_params=pltpu.CompilerParams(
+            vmem_limit_bytes=56 << 20, collective_id=1, has_side_effects=True
+        ),
+        cost_estimate=cost(60e9, 30 << 20),
+        name="factor",
+    )(block, panel_rows)
     vmem = pl.BlockSpec(memory_space=pltpu.VMEM)
     hbm = pl.BlockSpec(memory_space=pl.ANY)
     smem = pl.BlockSpec(memory_space=pltpu.SMEM)
@@ -654,7 +733,6 @@
         ri=(tiles, LIVE, LIVE),
         q=(tiles, LIVE, width),
     )
-    devices = lax.axis_size("row")
     mid = pl.pallas_call(
         prepare_kernel,
         in_specs=[smem] * 4 + [hbm] * 3 + [vmem] * 3 + [hbm],

time: 137 us -> 130 us (0.949)
  between operations: 14.1 us -> 0.68 us
  Pallas kernels: 120 us -> 127 us
    pallas_call x2 -> x1, Pallas kernels: 82.5 us -> 89.6 us  [on_device(): pl.pallas_call(factor_kernel, in_specs=[pl.BlockSpec(memory_space=pl.ANY)...]
  transfers between devices with their start and end apart: 1 -> 0, of which waited for: 0 -> 0; matrix products, arithmetic and copies ran while one was open for 2% -> 0% of each run, Pallas kernels for 60% -> 0%
where the time goes in v5:
time: 130 us
  Pallas kernels  127 us (98%)
  local copies, waits for them, and re-layouts  1.78 us (1%)
    pallas_call x1, Pallas kernels, on_device(): pl.pallas_call(factor_kernel, in_specs=[pl.BlockSpec(memory_space=pl.ANY)...  89.6 us
    pallas_call x1, Pallas kernels, on_device(): pl.pallas_call(prepare_kernel, in_specs=[smem] * 4 + [hbm] * 3 + [vmem] *...  17.8 us
    pallas_call x1, Pallas kernels, on_device(): pl.pallas_call(finish_kernel, grid=(tiles,), in_specs=[smem, pl.BlockSpec...  11 us
    pallas_call x1, Pallas kernels, on_device(): pl.pallas_call(column_kernel, grid=(1,), in_specs=[whole(gathered.shape),...  8.7 us

profile of v5, /device:TPU:1, one launch (start us, length us, event | category | flops | bytes accessed | tf_op | source)
XLA Modules:
  0.0 130.2 jit_solution(17168246334840832309)
XLA Ops:
  0.0 0.9 slice_bitcast_fusion
  0.9 0.9 copy.12
  1.8 0.7 pad_maximum_fusion.x_ref
  2.5 89.6 %factor.1 = (f32[32,48,1024]{2,1,0:T(8,128)}, f32[8,2,8,64,128]{4,3,2,1,0:T(8,128)}, f32[1024,1024]{1,0:T(8,128)}) custom-call(f32[48,1024]{1,0:T(8,128)} %pad_maximum_fusion.x_ref, f32[2,8,64,128]{3,2,1,0:T(8,128)} %panel_ref.1), custom_call_target="tpu_custom_call" | custom-call | flops 60000002048 | bytes 31457280 | tf_op jit(solution)/shard_map/factor/pallas_call | solution.py:678
  92.1 8.7 %columns.1 = (f32[64,1024]{1,0:T(8,128)}, f32[2,64,1024]{2,1,0:T(8,128)}, f32[32,192]{1,0:T(8,128)}, f32[8,64,1024]{2,1,0:T(8,128)}) custom-call(f32[32,48,1024]{2,1,0:T(8,128)} %get-tuple-element.18.g_ref, f32[8,2,8,64,128]{4,3,2,1,0:T(8,128)} %get-tuple-element.17.rows_ref.rows_hbm, f32[1024,1024]{1,0:T(8,128)} %get-tuple-element.19.inv_ref, ...), custom_call_target="tpu_custom_call" | custom-call | flops 2000000000 | bytes 6291456 | tf_op jit(solution)/shard_map/columns/pallas_call | solution.py:719
  101.4 17.8 %prepare.1 = (f32[2,4,64,64]{3,2,1,0:T(8,128)}, f32[2,4,32,64]{3,2,1,0:T(8,128)}, f32[2,4,32,64]{3,2,1,0:T(8,128)}, f32[2,32,32]{2,1,0:T(8,128)}, f32[2,32,1024]{2,1,0:T(8,128)}) custom-call(s32[2]{0:T(128)} %prank_ref.1, s32[1]{0:T(128)S(6)} %copy.13.crank_ref, s32[2]{0:T(128)} %bitcast.13, s32[2]{0:T(128)} %bitcast.12, ...), custom_call_target="tpu_custom_call" | custom-call | flops 10000000000 | bytes 20971520 | tf_op jit(solution)/shard_map/prepare/pallas_call | solution.py:736
  119.2 11.0 %finish.1 = f32[2,1,8,64,1024]{4,3,2,1,0:T(8,128)} custom-call(s32[2]{0:T(128)} %bitcast.14, f32[8,2,8,64,128]{4,3,2,1,0:T(8,128)} %get-tuple-element.17.rows_ref.rows_hbm, f32[8,64,1024]{2,1,0:T(8,128)} %get-tuple-element.20.cols_hbm.cols_ref, f32[2,1,8,64,1024]{4,3,2,1,0:T(8,128)} %tr_ref.1, f32[2,4,64,64]{3,2,1,0:T(8,128)} %get-tuple-element.24.w_ref, ...), custom_call_target="tpu_custom_call" | custom-call | flops 10000000000 | bytes 20971520 | tf_op jit(solution)/shard_map/finish/pallas_call | solution.py:759
